TPU v7x, 32 devices: a whole 2x2x4 slice. The times are simulated.
32 devices in a mesh: tm: 8 (over y, x, core), chan: 4 (over z).
Axes of the slice: x: 2, y: 2, z: 4, core: 2. Of those that a mesh axis runs over, the one named last changes fastest.
Arguments:
- frames: bfloat16 [8192, 1280], P('tm', 'chan'), may hold values from -64 to 64
- up_weight: bfloat16 [1280, 5120], P('tm', 'chan'), may hold values from -0.15625 to 0.15625
- down_weight: bfloat16 [5120, 1280], P('chan', 'tm'), may hold values from -0.078125 to 0.078125
- ffn_gain: float32 [1280], replicated, may hold values from 0.1 to 1.9
- final_gain: float32 [1280], replicated, may hold values from 0.5 to 1.5
- ctc_weight: bfloat16 [1280, 256], replicated, may hold values from -12 to 12
- labels: int32 [8192], replicated, may hold values from 0 to 255, as said below
- starts: int32 [32], replicated, may hold values from 0 to 1984, as said below
- widths: int32 [32], replicated, may hold values from 64 to 128
Outputs:
- emissions: float32 [8192, 256], P(('tm', 'chan'))
- band_scores: float32 [32, 128], P(('tm', 'chan'))
Inputs may be any that keep to these rules, and one draw needn't show every extreme that they name: `labels`: every even state has id 0. Never falling; starts[0] and each rise from one entry to the next are at most 128; the last entry is the largest.
All inputs are finite; a program needn't handle non-finite values.
Results may differ from a plain program's by a relative error of at most 0.0023.
Values may be sent and summed in bfloat16 or wider, within the bound.
No kernel may reach another device: no remote copies, remote signals or barrier semaphores. Data moves between devices by JAX's collectives and lax.ppermute only.
A program may use at most 64 MiB of HBM per device.

v0:
```python
import functools

import jax
import jax.numpy as jnp
from jax import lax
from jax.experimental import pallas as pl
from jax.experimental.pallas import tpu as pltpu
from jax.sharding import PartitionSpec as P


BAND = 128
RING = 2 * BAND
LANES = 128
PHASES = 8
LANE_STATES = RING // PHASES
LANE_ROWS = LANES // LANE_STATES
LN_EPSILON = 1e-05
NEG_SCORE = -1000000000.0
CHUNKS = 2
VMEM_LIMIT = 24 * 1024 * 1024
FFN_VMEM = 40 * 1024 * 1024


f32 = jnp.float32
bf16 = jnp.bfloat16


def line_gather(x, n):
    r1 = lax.ppermute(x, "chan", [(i, i + 1) for i in range(n - 1)])
    l1 = lax.ppermute(x, "chan", [(i + 1, i) for i in range(n - 1)])
    r2 = []
    l2 = []
    for k in range(1, n - 1):
        r2.append(lax.ppermute(r1, "chan", [(i, i + k) for i in range(1, n - k)]))
        l2.append(lax.ppermute(l1, "chan", [(i, i - k) for i in range(k, n - 1)]))
    return [x, r1, l1, *r2, *l2]


def piece_at(a, z, n):
    if a == z:
        return 0
    if a == z - 1:
        return 1
    if a == z + 1:
        return 2
    if a < z:
        return 3 + (z - a - 1) - 1
    return 3 + (n - 2) + (a - z - 1) - 1


def line_scatter(parts, n):
    right = parts[0].astype(f32)
    left = parts[n - 2].astype(f32)
    for k in range(1, n - 1):
        got = lax.ppermute(parts[k], "chan", [(i, i + k) for i in range(0, n - 1 - k)])
        right = right + got.astype(f32)
        got = lax.ppermute(parts[n - 2 - k], "chan", [(i, i - k) for i in range(k + 1, n)])
        left = left + got.astype(f32)
    from_left = lax.ppermute(right.astype(bf16), "chan", [(i, i + 1) for i in range(n - 1)])
    from_right = lax.ppermute(left.astype(bf16), "chan", [(i + 1, i) for i in range(n - 1)])
    return from_left, from_right


def tm_gather(x, size, bits):
    dist = [0]
    for b in bits:
        got = lax.ppermute(x, "tm", [(i, i ^ (1 << b)) for i in range(size)])
        x = jnp.concatenate([x, got], axis=0)
        dist = dist + [d ^ (1 << b) for d in dist]
    got = lax.ppermute(x, "tm", [(i, i ^ 1) for i in range(size)])
    return x, got, dist


def prepare_kernel(dist, meta, *refs):
    ups, dns = refs[0:2], refs[2:4]
    up_t, dn_t, up, usem, dsem = refs[4:]
    up_dist, dn_dist = dist
    tall = ups[0].shape[0] // len(up_dist)
    me = meta[1]

    def copies(srcs, dst, sem, dist):
        made = []
        for core in range(2):
            for q, d in enumerate(dist):
                row = pl.multiple_of(lax.bitwise_xor(me, d ^ core) * tall, 16)
                made.append(
                    pltpu.make_async_copy(
                        srcs[core].at[pl.ds(q * tall, tall)],
                        dst.at[pl.ds(row, tall)],
                        sem.at[core * len(dist) + q],
                    )
                )
        return made

    up_copies = copies(ups, up, usem, up_dist)
    dn_copies = copies(dns, dn_t, dsem, dn_dist)
    for c in up_copies + dn_copies:
        c.start()
    for c in up_copies:
        c.wait()
    step = 256
    for i in range(0, up.shape[0], step):
        for j in range(0, up.shape[1], step):
            wide = min(step, up.shape[1] - j)
            up_t[j : j + wide, i : i + step] = up[i : i + step, j : j + wide].T
    for c in dn_copies:
        c.wait()


def prepare(meta, ups, dns, dist, width):
    hidden = ups[0].shape[1]
    count = 2 * len(dist[0])
    vmem = pl.BlockSpec(memory_space=pltpu.VMEM)
    anywhere = pl.BlockSpec(memory_space=pl.ANY)
    return pl.pallas_call(
        functools.partial(prepare_kernel, dist),
        out_shape=[
            jax.ShapeDtypeStruct((hidden, width), bf16),
            jax.ShapeDtypeStruct((width, hidden), bf16),
        ],
        in_specs=[pl.BlockSpec(memory_space=pltpu.SMEM)] + [anywhere] * 4,
        out_specs=[vmem] * 2,
        scratch_shapes=[
            pltpu.VMEM((width, hidden), bf16),
            pltpu.SemaphoreType.DMA((count,)),
            pltpu.SemaphoreType.DMA((count,)),
        ],
        compiler_params=pltpu.CompilerParams(vmem_limit_bytes=VMEM_LIMIT),
        cost_estimate=pl.CostEstimate(
            flops=0, bytes_accessed=8 * width * hidden, transcendentals=0
        ),
        name="prepare",
    )(meta, *ups, *dns)


def ffn_kernel(n, chunk, chunks, meta, gain, up_hbm, dn_hbm, *refs):
    pieces = 1 + 2 + 2 * (n - 2)
    xs = refs[:pieces]
    outs = refs[pieces : pieces + n]
    xin, xn, hid, up_t, dn_t, terms, base, xsem, wsem, osem = refs[pieces + n :]
    width, rows = xin.shape
    feat = width // n
    fc = rows // n
    z = meta[0]
    for a in range(n):
        for here in range(n):

            @pl.when(z == here)
            def _(a=a, here=here):
                for r in range(n):
                    column = (((here + r) % n) * chunks + chunk) * fc
                    pltpu.make_async_copy(
                        xs[piece_at(a, here, n)].at[:, pl.ds(column, fc)],
                        xin.at[pl.ds(a * feat, feat), pl.ds(r * fc, fc)],
                        xsem.at[a * n + r],
                    ).start()

    up_copy = pltpu.make_async_copy(up_hbm, up_t, wsem.at[0])
    dn_copy = pltpu.make_async_copy(dn_hbm, dn_t, wsem.at[1])
    up_copy.start()
    dn_copy.start()

    for r in range(n):
        for a in range(n):
            pltpu.make_async_copy(
                xs[0].at[:, pl.ds(0, fc)],
                xin.at[pl.ds(a * feat, feat), pl.ds(r * fc, fc)],
                xsem.at[a * n + r],
            ).wait()
    up_copy.wait()
    hidden = up_t.shape[0]
    step = 256 if hidden % 256 == 0 else 128
    half = max(rows // 2, 256)
    for start in range(0, rows, half):
        for h in range(start, start + half, 128):
            x = xin[:, h : h + 128].astype(f32)
            mean = jnp.mean(x, axis=0, keepdims=True)
            var = jnp.mean(jnp.square(x - mean), axis=0, keepdims=True)
            normed = (x - mean) * lax.rsqrt(var + LN_EPSILON) * gain[...]
            xn[:, h : h + 128] = normed.astype(bf16)
        for j in range(0, hidden, step):
            a = jnp.dot(
                up_t[j : j + step, :], xn[:, start : start + half], preferred_element_type=f32
            )
            hid[j : j + step, start : start + half] = (a / (1.0 + jnp.exp(-a))).astype(bf16)
    dn_copy.wait()
    copies = []
    for k, j in enumerate(range(0, width, 256)):
        p = jnp.dot(dn_t[j : j + 256, :], hid[...], preferred_element_type=f32)
        for r in range(n):
            term = p[:, r * fc : (r + 1) * fc]
            if r == 0:
                base[j : j + 256, :] = xin[j : j + 256, :fc].astype(f32) + 0.5 * term
                src = base.at[pl.ds(j, 256)]
            else:
                terms[r - 1, j : j + 256, :] = term.astype(bf16)
                src = terms.at[r - 1, pl.ds(j, 256)]
            copy = pltpu.make_async_copy(
                src, outs[(r - 1) % n].at[pl.ds(j, 256)], osem.at[k * n + r]
            )
            copy.start()
            copies.append(copy)
    for copy in copies:
        copy.wait()


def ffn(meta, gain, up_t, dn_t, xs, n, chunk, chunks):
    _, rows = xs[0].shape
    rows = rows // chunks
    fc = rows // n
    hidden, width = up_t.shape
    vmem = pl.BlockSpec(memory_space=pltpu.VMEM)
    anywhere = pl.BlockSpec(memory_space=pl.ANY)
    return pl.pallas_call(
        functools.partial(ffn_kernel, n, chunk, chunks),
        out_shape=[jax.ShapeDtypeStruct((width, fc), bf16)] * (n - 1)
        + [jax.ShapeDtypeStruct((width, fc), f32)],
        in_specs=[pl.BlockSpec(memory_space=pltpu.SMEM), vmem] + [anywhere] * (2 + len(xs)),
        out_specs=[anywhere] * n,
        scratch_shapes=[
            pltpu.VMEM((width, rows), bf16),
            pltpu.VMEM((width, rows), bf16),
            pltpu.VMEM((hidden, rows), bf16),
            pltpu.VMEM((hidden, width), bf16),
            pltpu.VMEM((width, hidden), bf16),
            pltpu.VMEM((n - 1, width, fc), bf16),
            pltpu.VMEM((width, fc), f32),
            pltpu.SemaphoreType.DMA((n * n,)),
            pltpu.SemaphoreType.DMA((2,)),
            pltpu.SemaphoreType.DMA((n * (width // 256),)),
        ],
        compiler_params=pltpu.CompilerParams(vmem_limit_bytes=FFN_VMEM),
        cost_estimate=pl.CostEstimate(
            flops=4 * rows * width * hidden,
            bytes_accessed=4 * width * hidden + 6 * rows * width,
            transcendentals=rows * hidden,
        ),
        name="ffn",
    )(meta, gain, up_t, dn_t, *xs)


def band_states(shard, starts, widths):
    prior = jnp.maximum(shard - 1, 0)
    start_in = jnp.where(shard > 0, starts[prior], 0)
    width_in = jnp.where(shard > 0, widths[prior], 2)
    return start_in, width_in, starts[shard], widths[shard]


def tail_kernel(first, last, meta, starts, widths, base, left, right, gain, ctc_t, label_rows, *refs):
    if not first:
        state_in, refs = refs[0], refs[1:]
    emit, state_out, gaps = refs
    start_in, width_in, start_out, width_out = band_states(meta[2], starts, widths)

    residual = base[...] + 0.5 * (left[...].astype(f32) + right[...].astype(f32))
    mean = jnp.mean(residual, axis=0, keepdims=True)
    var = jnp.mean(jnp.square(residual - mean), axis=0, keepdims=True)
    normed = ((residual - mean) * lax.rsqrt(var + LN_EPSILON) * gain[...]).astype(bf16)
    logits = jnp.dot(ctc_t[...], normed, preferred_element_type=f32)
    logits = logits - jnp.max(logits, axis=0, keepdims=True)
    emissions = (logits - jnp.log(jnp.sum(jnp.exp(logits), axis=0, keepdims=True))).T
    emit[...] = emissions

    odd_start = lax.rem(start_in, 2)
    origin = start_in - odd_start
    row = start_in // RING
    after = jnp.minimum(row + 1, label_rows.shape[0] - 1)
    ring = row * RING + lax.broadcasted_iota(jnp.int32, (8, RING), 1)
    around = jnp.where(
        ring >= start_in,
        jnp.broadcast_to(label_rows[pl.ds(row, 1), :], (8, RING)),
        jnp.broadcast_to(label_rows[pl.ds(after, 1), :], (8, RING)),
    )
    lane = lax.broadcasted_iota(jnp.int32, (8, LANES), 1)
    sub = lax.broadcasted_iota(jnp.int32, (8, LANES), 0)
    spot = lax.rem(lane, LANE_STATES)
    block = lane // LANE_STATES
    odd_phases = list(range(1, PHASES, 2))

    shape = (RING, LANES * len(odd_phases))
    held = lax.broadcasted_iota(jnp.int32, shape, 1)
    held = origin + PHASES * lax.rem(held, LANE_STATES) + 2 * (held // LANES) + 1
    pick = lax.broadcasted_iota(jnp.int32, shape, 0) == lax.rem(held, RING)
    ids = jnp.dot(
        around.astype(f32).astype(bf16), pick.astype(f32).astype(bf16), preferred_element_type=f32
    ).astype(jnp.int32)
    ids_of = {p: ids[:, LANES * k : LANES * (k + 1)] for k, p in enumerate(odd_phases)}
    skip = {}
    for p in odd_phases:
        if p == 1:
            behind = pltpu.roll(ids_of[PHASES - 1], 1, axis=1)
        else:
            behind = ids_of[p - 2]
        skip[p] = (PHASES * spot + p - odd_start >= 2) & (ids_of[p] != behind)
    no_back = (spot == 0) & (odd_start == 0)
    no_rise = (spot == 0) & (odd_start == 1)

    vocab = emissions.shape[1]
    choose = (
        lax.broadcasted_iota(jnp.int32, (vocab, shape[1]), 0)
        == jnp.broadcast_to(ids[0:1], (vocab, shape[1]))
    )
    choose = choose.astype(f32).astype(bf16)
    rest = emissions
    picked = jnp.zeros((emissions.shape[0], shape[1]), f32)
    for _ in range(3):
        part = rest.astype(bf16)
        rest = rest - part.astype(f32)
        picked = picked + jnp.dot(part, choose, preferred_element_type=f32)
    blank = emissions[:, 0:1]
    gaps[...] = picked - blank
    blank_total = jnp.sum(blank)

    groups = BAND // (8 * LANE_ROWS)
    if first:
        rows = []
        for g in range(groups):
            entry = g * 8 * LANE_ROWS + 8 * block + sub
            for p in range(PHASES):
                state = origin + PHASES * spot + p
                live = (state >= start_in) & (state < start_in + jnp.minimum(width_in, BAND))
                rows.append(jnp.where(live & (lax.rem(state, BAND) == entry), 0.0, NEG_SCORE))
    else:
        rows = [state_in[k] for k in range(groups * PHASES)]

    def steps(t, rows):
        rows = list(rows)
        start = pl.multiple_of(t * 8, 8)
        tiles = {
            p: gaps[pl.ds(start, 8), LANES * k : LANES * (k + 1)] for k, p in enumerate(odd_phases)
        }
        for u in range(8):
            gap = {p: jnp.broadcast_to(tiles[p][u : u + 1], (8, LANES)) for p in odd_phases}
            for g in range(groups):
                was = rows[g * PHASES : (g + 1) * PHASES]
                now = list(was)
                back = jnp.where(no_back, NEG_SCORE, pltpu.roll(was[PHASES - 1], 1, axis=1))
                for p in range(0, PHASES, 2):
                    now[p] = jnp.maximum(was[p], back if p == 0 else was[p - 1])
                for p in odd_phases:
                    come = jnp.where(skip[p], now[p - 1], was[p - 1])
                    if p == 1:
                        come = jnp.where(no_rise, NEG_SCORE, come)
                    now[p] = jnp.maximum(was[p], come) + gap[p]
                rows[g * PHASES : (g + 1) * PHASES] = now
        return tuple(rows)

    rows = lax.fori_loop(0, emissions.shape[0] // 8, steps, tuple(rows))
    if not last:
        for k in range(groups * PHASES):
            state_out[k] = rows[k] + blank_total
        return

    stack = jnp.concatenate(
        [
            jnp.concatenate([rows[g * PHASES + p] for p in range(PHASES)], axis=1)
            for g in range(groups)
        ],
        axis=0,
    )
    parts = []
    for _ in range(3):
        part = stack.astype(bf16)
        stack = stack - part.astype(f32)
        parts.append(part.astype(f32))
    parts = jnp.concatenate(parts, axis=0).astype(bf16)
    count = groups * 8
    where = lax.broadcasted_iota(jnp.int32, (PHASES * LANES, 1), 0)
    slot = lax.rem(where, LANES)
    state = origin + PHASES * lax.rem(slot, LANE_STATES) + where // LANES
    owner = slot // LANE_STATES
    beyond = (state == origin) & (odd_start == 1)
    state = jnp.where(beyond, origin + RING, state)
    owner = jnp.where(beyond, lax.rem(owner + LANE_ROWS - 1, LANE_ROWS), owner)
    leaves = (state >= start_out) & (state < start_out + BAND)
    column = jnp.where(leaves, lax.rem(state, BAND), -1)
    wanted = lax.broadcasted_iota(jnp.int32, (PHASES * LANES, BAND), 1)
    exit_residue = lax.broadcasted_iota(jnp.int32, (8, BAND), 1)
    ahead = lax.rem(exit_residue - lax.rem(start_out, BAND) + BAND, BAND)
    for e in range(LANE_ROWS):
        take = jnp.where(owner == e, column, -1) == wanted
        got = jnp.dot(parts, take.astype(f32).astype(bf16), preferred_element_type=f32)
        got = got[:count] + got[count : 2 * count] + got[2 * count :]
        for g in range(groups):
            first_row = g * 8 * LANE_ROWS + 8 * e
            state_out[first_row : first_row + 8, :] = jnp.where(
                ahead < width_out, got[8 * g : 8 * g + 8] + blank_total, NEG_SCORE
            )


def tail(first, last, meta, starts, widths, base, left, right, gain, ctc_t, label_rows, *state):
    fc = base.shape[1]
    vocab = ctc_t.shape[0]
    smem = pl.BlockSpec(memory_space=pltpu.SMEM)
    vmem = pl.BlockSpec(memory_space=pltpu.VMEM)
    shape = (BAND, BAND) if last else (RING * BAND // (8 * LANES), 8, LANES)
    return pl.pallas_call(
        functools.partial(tail_kernel, first, last),
        out_shape=[jax.ShapeDtypeStruct((fc, vocab), f32), jax.ShapeDtypeStruct(shape, f32)],
        in_specs=[smem] * 3 + [vmem] * (6 + len(state)),
        out_specs=[vmem] * 2,
        scratch_shapes=[pltpu.VMEM((fc, LANES * PHASES // 2), f32)],
        compiler_params=pltpu.CompilerParams(vmem_limit_bytes=VMEM_LIMIT),
        cost_estimate=pl.CostEstimate(
            flops=40 * fc * BAND * BAND, bytes_accessed=16 * fc * gain.shape[0], transcendentals=fc * vocab
        ),
        name="tail",
    )(meta, starts, widths, base, left, right, gain, ctc_t, label_rows, *state)


def product_kernel(mats, out, left):
    groups = BAND // 8
    out[...] = mats[0]

    def lap(k, _):
        left[...] = out[...]

        def block(j, acc):
            shift = lax.rem(BAND - 8 * j, BAND)
            terms = [
                pltpu.roll(left[8 * g : 8 * g + 8, :], shift, axis=1) for g in range(groups)
            ]
            later = mats[k, pl.ds(pl.multiple_of(8 * j, 8), 8), :]
            acc = list(acc)
            for u in range(8):
                row = jnp.broadcast_to(later[u : u + 1], (8, BAND))
                for g in range(groups):
                    col = jnp.broadcast_to(terms[g][:, u : u + 1], (8, BAND))
                    acc[g] = jnp.maximum(acc[g], col + row)
            return tuple(acc)

        none = jnp.full((8, BAND), 64 * NEG_SCORE, f32)
        acc = lax.fori_loop(0, BAND // 8, block, (none,) * groups)
        for g in range(groups):
            out[8 * g : 8 * g + 8, :] = acc[g]
        return 0

    lax.fori_loop(1, mats.shape[0], lap, 0)


def product(mats):
    vmem = pl.BlockSpec(memory_space=pltpu.VMEM)
    return pl.pallas_call(
        product_kernel,
        out_shape=jax.ShapeDtypeStruct((BAND, BAND), f32),
        in_specs=[vmem],
        out_specs=vmem,
        scratch_shapes=[pltpu.VMEM((BAND, BAND), f32)],
        compiler_params=pltpu.CompilerParams(vmem_limit_bytes=VMEM_LIMIT),
        name="product",
    )(mats)


def score_kernel(scale, meta, starts, widths, near, far, out):
    z = meta[0]
    me = meta[1]
    _, _, start_out, width_out = band_states(meta[2], starts, widths)
    sub = lax.broadcasted_iota(jnp.int32, (BAND, BAND), 0)
    lane = lax.broadcasted_iota(jnp.int32, (BAND, BAND), 1)

    def through(col, mat):
        return jnp.max(col + mat, axis=0, keepdims=True)

    def turn(row):
        return jnp.max(
            jnp.where(sub == lane, jnp.broadcast_to(row, (BAND, BAND)), 64 * NEG_SCORE),
            axis=1,
            keepdims=True,
        )

    place = lax.broadcasted_iota(jnp.int32, (BAND, 1), 0)
    col = jnp.where(place < 2, 0.0, NEG_SCORE).astype(f32)
    col = lax.fori_loop(0, me, lambda g, c: turn(through(c, far[g])), col)
    col = lax.fori_loop(0, z, lambda k, c: turn(through(c, near[k])), col)
    col = turn(through(col, near[z]))
    home = lax.rem(start_out + lane, BAND)
    best = jnp.max(jnp.where(sub == home, col, 64 * NEG_SCORE), axis=0, keepdims=True)
    live = lax.broadcasted_iota(jnp.int32, (1, BAND), 1) < width_out
    out[...] = jnp.where(live, best * scale, 0.0)


def scores(scale, meta, starts, widths, near, far):
    smem = pl.BlockSpec(memory_space=pltpu.SMEM)
    vmem = pl.BlockSpec(memory_space=pltpu.VMEM)
    return pl.pallas_call(
        functools.partial(score_kernel, scale),
        out_shape=jax.ShapeDtypeStruct((1, BAND), f32),
        in_specs=[smem] * 3 + [vmem] * 2,
        out_specs=vmem,
        compiler_params=pltpu.CompilerParams(vmem_limit_bytes=VMEM_LIMIT),
        name="scores",
    )(meta, starts, widths, near, far)


def compute(frames, up_weight, down_weight, ffn_gain, final_gain, ctc_weight, labels, starts, widths):
    n = lax.axis_size("chan")
    z = lax.axis_index("chan")
    size = lax.axis_size("tm")
    me = lax.axis_index("tm")
    rows, feat = frames.shape
    shard = me * n + z
    meta = jnp.stack([z, me, shard]).astype(jnp.int32)
    high = list(range(1, size.bit_length() - 1))
    label_rows = labels.reshape(-1, RING)
    gain = ffn_gain.reshape(-1, 1)
    last_gain = final_gain.reshape(-1, 1)
    ctc_t = ctc_weight.T

    gathered = line_gather(frames.T, n)
    up_own, up_other, dist = tm_gather(up_weight, size, high)
    dn_own, dn_other, dn_dist = tm_gather(down_weight.T, size, high[::-1])
    up_t, dn_t = prepare(
        meta, (up_own, up_other), (dn_own, dn_other), (dist, dn_dist), n * feat
    )

    state = ()
    emitted = []
    for c in range(CHUNKS):
        *parts, base = ffn(meta, gain, up_t, dn_t, gathered, n, c, CHUNKS)
        from_left, from_right = line_scatter(parts, n)
        emissions, state = tail(
            c == 0,
            c == CHUNKS - 1,
            meta,
            starts,
            widths,
            base,
            from_left,
            from_right,
            last_gain,
            ctc_t,
            label_rows,
            *((state,) if c else ()),
        )
        emitted.append(emissions)
    emissions = jnp.concatenate(emitted, axis=0) if CHUNKS > 1 else emitted[0]

    near = lax.all_gather(state, "chan")
    far = lax.all_gather(product(near), "tm")
    band_row = scores(1.0 / (rows * size), meta, starts, widths, near, far)
    return emissions, band_row


def solution(mesh):
    in_specs = (P("tm", "chan"), P("tm", "chan"), P("chan", "tm"), P(), P(), P(), P(), P(), P())
    out_specs = (P(("tm", "chan"), None), P(("tm", "chan"), None))
    return jax.shard_map(compute, mesh=mesh, in_specs=in_specs, out_specs=out_specs, check_vma=False)
```

profile of v0, /device:TPU:0, one launch (start us, length us, event | category | flops | bytes accessed | tf_op | source)
XLA Modules:
  0.0 232.1 jit_solution(6199699016251767911)
XLA Ops:
  0.6 3.1 %collective-permute-start.3 = (bf16[160,1280]{1,0:T(8,128)(2,1)}, bf16[160,1280]{1,0:T(8,128)(2,1)S(1)}, u32[]{:S(2)}, u32[]{:S(2)}) collective-permute-start(bf16[160,1280]{1,0:T(8,128)(2,1)} %bitcast.17), channel_id=1, source_target_pairs={{0,16},{4,20},{8,24},{12,28},{16,0},{20,4},{24,8},{28,12},{1,17},{... | collective-permute-start | bytes 1228808 | tf_op jit(solution)/shard_map/ppermute | solution.py:67
  3.7 9.7 %collective-permute-done.3 = bf16[160,1280]{1,0:T(8,128)(2,1)S(1)} collective-permute-done((bf16[160,1280]{1,0:T(8,128)(2,1)}, bf16[160,1280]{1,0:T(8,128)(2,1)S(1)}, u32[]{:S(2)}, u32[]{:S(2)}) %collective-permute-start.3) | collective-permute-done | bytes 409632 | tf_op jit(solution)/shard_map/ppermute | solution.py:67
  14.4 1.8 collective-permute-start.4
  16.5 26.2 %collective-permute-done = bf16[160,1280]{1,0:T(8,128)(2,1)S(1)} collective-permute-done((bf16[160,1280]{1,0:T(8,128)(2,1)S(1)}, bf16[160,1280]{1,0:T(8,128)(2,1)S(1)}, u32[]{:S(2)}, u32[]{:S(2)}) %collective-permute-start) | collective-permute-done | bytes 409632 | tf_op jit(solution)/shard_map/ppermute | solution.py:67
  42.8 1.5 collective-permute-start.1
  44.6 16.8 %collective-permute-done.1 = bf16[320,1280]{1,0:T(8,128)(2,1)S(1)} collective-permute-done((bf16[320,1280]{1,0:T(8,128)(2,1)S(1)}, bf16[320,1280]{1,0:T(8,128)(2,1)S(1)}, u32[]{:S(2)}, u32[]{:S(2)}) %collective-permute-start.1) | collective-permute-done | bytes 819232 | tf_op jit(solution)/shard_map/ppermute | solution.py:67
  61.5 1.3 collective-permute-start.7
  62.8 5.4 %collective-permute-start.6 = (bf16[320,1024]{1,0:T(8,128)(2,1)S(1)}, bf16[320,1024]{1,0:T(8,128)(2,1)}, u32[]{:S(2)}, u32[]{:S(2)}) collective-permute-start(bf16[320,1024]{1,0:T(8,128)(2,1)S(1)} %bitcast.14), channel_id=1, source_target_pairs={{0,1},{1,2},{2,3},{4,5},{5,6},{6,7},{8,9},{9,10},{10,11},{12,13},{... | collective-permute-start | bytes 1966088 | tf_op jit(solution)/shard_map/ppermute | solution.py:29
  68.2 12.4 %collective-permute-done.7.refs_2_ = bf16[320,1024]{1,0:T(8,128)(2,1)} collective-permute-done((bf16[320,1024]{1,0:T(8,128)(2,1)S(1)}, bf16[320,1024]{1,0:T(8,128)(2,1)}, u32[]{:S(2)}, u32[]{:S(2)}) %collective-permute-start.7) | collective-permute-done | bytes 655392 | tf_op jit(solution)/shard_map/ppermute | solution.py:30
  80.6 1.3 collective-permute-start.10
  81.9 1.3 collective-permute-start.11
  83.2 1.5 collective-permute-start.8
  85.9 1.5 collective-permute-start.9
  88.6 1.4 copy-done.1
  90.1 4.1 %prepare.1 = (bf16[1280,1280]{1,0:T(8,128)(2,1)S(1)}, bf16[1280,1280]{1,0:T(8,128)(2,1)S(1)}) custom-call(s32[3]{0:T(128)S(1)} %pad_add_fusion.meta, bf16[640,1280]{1,0:T(8,128)(2,1)S(1)} %constant_dynamic-update-slice_fusion.refs_0_, bf16[640,1280]{1,0:T(8,128)(2,1)} %collective-permute-done.2.refs_1_, bf16[640,1280]{1,0:T(8,128)(2,1)S(1)} %pad_maximum_fusion.refs_2_, ...), custom_call_target="tpu_custom_call" | custom-call | bytes 13107200 | tf_op jit(solution)/shard_map/prepare/pallas_call | solution.py:115
  94.2 5.6 %collective-permute-done.10.refs_5_ = bf16[320,1024]{1,0:T(8,128)(2,1)} collective-permute-done((bf16[320,1024]{1,0:T(8,128)(2,1)}, bf16[320,1024]{1,0:T(8,128)(2,1)}, u32[]{:S(2)}, u32[]{:S(2)}) %collective-permute-start.10) | collective-permute-done | bytes 655392 | tf_op jit(solution)/shard_map/ppermute | solution.py:35
  99.8 14.0 %collective-permute-done.11.refs_6_ = bf16[320,1024]{1,0:T(8,128)(2,1)} collective-permute-done((bf16[320,1024]{1,0:T(8,128)(2,1)}, bf16[320,1024]{1,0:T(8,128)(2,1)}, u32[]{:S(2)}, u32[]{:S(2)}) %collective-permute-start.11) | collective-permute-done | bytes 655392 | tf_op jit(solution)/shard_map/ppermute | solution.py:35
  113.8 10.4 %ffn.2 = (bf16[1280,128]{1,0:T(8,128)(2,1)S(1)}, bf16[1280,128]{1,0:T(8,128)(2,1)S(1)}, bf16[1280,128]{1,0:T(8,128)(2,1)S(1)}, f32[1280,128]{1,0:T(8,128)S(1)}) custom-call(s32[3]{0:T(128)S(1)} %pad_add_fusion.meta, f32[1280,1]{1,0:T(8,128)S(1)} %copy-done.2, bf16[1280,1280]{1,0:T(8,128)(2,1)S(1)} %get-tuple-element.16.up_hbm, ...), custom_call_target="tpu_custom_call" | custom-call | flops 3355443200 | bytes 10485760 | tf_op jit(solution)/shard_map/ffn/pallas_call | solution.py:214
  125.6 7.8 %collective-permute-start.12 = (bf16[1280,128]{1,0:T(8,128)(2,1)S(1)}, bf16[1280,128]{1,0:T(8,128)(2,1)S(1)}, u32[]{:S(2)}, u32[]{:S(2)}) collective-permute-start(bf16[1280,128]{1,0:T(8,128)(2,1)S(1)} %get-tuple-element.20), channel_id=1, source_target_pairs={{0,1},{1,2},{4,5},{5,6},{8,9},{9,10},{12,13},{13,14},{16,17},{17,1... | collective-permute-start | bytes 983048 | tf_op jit(solution)/shard_map/ppermute | solution.py:55
  133.4 10.4 %ffn.3 = (bf16[1280,128]{1,0:T(8,128)(2,1)S(1)}, bf16[1280,128]{1,0:T(8,128)(2,1)S(1)}, bf16[1280,128]{1,0:T(8,128)(2,1)S(1)}, f32[1280,128]{1,0:T(8,128)S(1)}) custom-call(s32[3]{0:T(128)S(1)} %pad_add_fusion.meta, f32[1280,1]{1,0:T(8,128)S(1)} %copy-done.2, bf16[1280,1280]{1,0:T(8,128)(2,1)S(1)} %get-tuple-element.16.up_hbm, ...), custom_call_target="tpu_custom_call" | custom-call | flops 3355443200 | bytes 10485760 | tf_op jit(solution)/shard_map/ffn/pallas_call | solution.py:214
  144.4 4.5 %collective-permute-start.18 = (bf16[1280,128]{1,0:T(8,128)(2,1)S(1)}, bf16[1280,128]{1,0:T(8,128)(2,1)S(1)}, u32[]{:S(2)}, u32[]{:S(2)}) collective-permute-start(bf16[1280,128]{1,0:T(8,128)(2,1)S(1)} %get-tuple-element.25), channel_id=1, source_target_pairs={{0,1},{1,2},{4,5},{5,6},{8,9},{9,10},{12,13},{13,14},{16,17},{17,1... | collective-permute-start | bytes 983048 | tf_op jit(solution)/shard_map/ppermute | solution.py:55
  148.9 3.4 %collective-permute-start.13 = (bf16[1280,128]{1,0:T(8,128)(2,1)S(1)}, bf16[1280,128]{1,0:T(8,128)(2,1)S(1)}, u32[]{:S(2)}, u32[]{:S(2)}) collective-permute-start(bf16[1280,128]{1,0:T(8,128)(2,1)S(1)} %get-tuple-element.21), channel_id=1, source_target_pairs={{0,2},{4,6},{8,10},{12,14},{16,18},{20,22},{24,26},{28,30}} | collective-permute-start | bytes 983048 | tf_op jit(solution)/shard_map/ppermute | solution.py:55
  153.9 1.3 collective-permute-start.19
  155.2 8.9 %collective-permute-done.13 = bf16[1280,128]{1,0:T(8,128)(2,1)S(1)} collective-permute-done((bf16[1280,128]{1,0:T(8,128)(2,1)S(1)}, bf16[1280,128]{1,0:T(8,128)(2,1)S(1)}, u32[]{:S(2)}, u32[]{:S(2)}) %collective-permute-start.13) | collective-permute-done | bytes 327712 | tf_op jit(solution)/shard_map/ppermute | solution.py:55
  166.2 5.4 %collective-permute-start.14 = (bf16[1280,128]{1,0:T(8,128)(2,1)}, bf16[1280,128]{1,0:T(8,128)(2,1)}, u32[]{:S(2)}, u32[]{:S(2)}) collective-permute-start(bf16[1280,128]{1,0:T(8,128)(2,1)} %add_convert_fusion.3), channel_id=1, source_target_pairs={{0,1},{1,2},{2,3},{4,5},{5,6},{6,7},{8,9},{9,10},{10,11},{12,13},{... | collective-permute-start | bytes 983048 | tf_op jit(solution)/shard_map/ppermute | solution.py:59
  172.5 1.4 collective-permute-start.23
  174.8 5.3 %collective-permute-start.20 = (bf16[1280,128]{1,0:T(8,128)(2,1)}, bf16[1280,128]{1,0:T(8,128)(2,1)}, u32[]{:S(2)}, u32[]{:S(2)}) collective-permute-start(bf16[1280,128]{1,0:T(8,128)(2,1)} %add_convert_fusion.1), channel_id=1, source_target_pairs={{0,1},{1,2},{2,3},{4,5},{5,6},{6,7},{8,9},{9,10},{10,11},{12,13},{... | collective-permute-start | bytes 983048 | tf_op jit(solution)/shard_map/ppermute | solution.py:59
  180.7 5.4 %tail.2 = (f32[128,256]{1,0:T(8,128)S(1)}, f32[32,8,128]{2,1,0:T(8,128)S(1)}) custom-call(s32[3]{0:T(128)S(1)} %pad_add_fusion.meta, s32[32]{0:T(128)S(1)} %copy-done.3, s32[32]{0:T(128)S(1)} %copy-done.4, f32[1280,128]{1,0:T(8,128)S(1)} %get-tuple-element.18.base, bf16[1280,128]{1,0:T(8,128)(2,1)} %collective-permute-done.14.left, ...), custom_call_target="tpu_custom_call" | custom-call | flops 83886080 | bytes 2621440 | tf_op jit(solution)/shard_map/tail/pallas_call | solution.py:397
  186.1 6.4 %tail.3 = (f32[128,256]{1,0:T(8,128)S(1)}, f32[128,128]{1,0:T(8,128)S(1)}) custom-call(s32[3]{0:T(128)S(1)} %pad_add_fusion.meta, s32[32]{0:T(128)S(1)} %copy-done.3, s32[32]{0:T(128)S(1)} %copy-done.4, f32[1280,128]{1,0:T(8,128)S(1)} %get-tuple-element.23.base, bf16[1280,128]{1,0:T(8,128)(2,1)} %collective-permute-done.20.left, ...), custom_call_target="tpu_custom_call" | custom-call | flops 83886080 | bytes 2621440 | tf_op jit(solution)/shard_map/tail/pallas_call | solution.py:397
  192.5 14.0 %all-gather = f32[512,128]{1,0:T(8,128)S(1)} all-gather(f32[128,128]{1,0:T(8,128)S(1)} %get-tuple-element.29), channel_id=2, replica_groups=mesh['tm'=8,'chan'=4] {'chan'}, dimensions={0}, use_global_device_ids=true | all-gather | bytes 327680 | tf_op jit(solution)/shard_map/all_gather | solution.py:538
  206.5 13.8 %product.1 = f32[128,128]{1,0:T(8,128)S(1)} custom-call(f32[4,128,128]{2,1,0:T(8,128)S(1)} %bitcast.10), custom_call_target="tpu_custom_call" | custom-call | tf_op jit(solution)/shard_map/product/pallas_call | solution.py:443
  220.4 9.8 %all-gather.1 = f32[1024,128]{1,0:T(8,128)S(1)} all-gather(f32[128,128]{1,0:T(8,128)S(1)} %product.1), channel_id=3, replica_groups=mesh['tm'=8,'chan'=4] {'tm'}, dimensions={0}, use_global_device_ids=true | all-gather | bytes 589824 | tf_op jit(solution)/shard_map/all_gather | solution.py:539
  (67 shorter events, 14.1 us)
Async XLA Ops:
  0.6 15.6 %copy-start.8 = (bf16[160,1280]{1,0:T(8,128)(2,1)S(1)}, bf16[160,1280]{1,0:T(8,128)(2,1)}, u32[]{:S(2)}) copy-start(bf16[160,1280]{1,0:T(8,128)(2,1)} %param.10) | copy-start | bytes 1228804
  0.6 43.6 %copy-start.7 = (bf16[1280,160]{0,1:T(8,128)(2,1)S(1)}, bf16[1280,160]{0,1:T(8,128)(2,1)}, u32[]{:S(2)}) copy-start(bf16[1280,160]{0,1:T(8,128)(2,1)} %param.11) | copy-start | bytes 1228804
  0.6 12.7 %collective-permute-start.3 = (bf16[160,1280]{1,0:T(8,128)(2,1)}, bf16[160,1280]{1,0:T(8,128)(2,1)S(1)}, u32[]{:S(2)}, u32[]{:S(2)}) collective-permute-start(bf16[160,1280]{1,0:T(8,128)(2,1)} %bitcast.17), channel_id=1, source_target_pairs={{0,16},{4,20},{8,24},{12,28},{16,0},{20,4},{24,8},{28,12},{1,17},{... | collective-permute-start | bytes 1228808 | tf_op jit(solution)/shard_map/ppermute | solution.py:67
  14.4 29.8 %collective-permute-start.4 = (bf16[320,1280]{1,0:T(8,128)(2,1)S(1)}, bf16[320,1280]{1,0:T(8,128)(2,1)S(1)}, u32[]{:S(2)}, u32[]{:S(2)}) collective-permute-start(bf16[320,1280]{1,0:T(8,128)(2,1)S(1)} %pad_maximum_fusion.2), channel_id=1, source_target_pairs={{0,8},{4,12},{8,0},{12,4},{16,24},{20,28},{24,16},{28,20},{1,9},{5... | collective-permute-start | bytes 2457608 | tf_op jit(solution)/shard_map/ppermute | solution.py:67
  16.2 26.5 %collective-permute-start = (bf16[160,1280]{1,0:T(8,128)(2,1)S(1)}, bf16[160,1280]{1,0:T(8,128)(2,1)S(1)}, u32[]{:S(2)}, u32[]{:S(2)}) collective-permute-start(bf16[160,1280]{1,0:T(8,128)(2,1)S(1)} %copy-done.8), channel_id=1, source_target_pairs={{0,8},{4,12},{8,0},{12,4},{16,24},{20,28},{24,16},{28,20},{1,9},{5... | collective-permute-start | bytes 1228808 | tf_op jit(solution)/shard_map/ppermute | solution.py:67
  42.8 18.6 %collective-permute-start.1 = (bf16[320,1280]{1,0:T(8,128)(2,1)S(1)}, bf16[320,1280]{1,0:T(8,128)(2,1)S(1)}, u32[]{:S(2)}, u32[]{:S(2)}) collective-permute-start(bf16[320,1280]{1,0:T(8,128)(2,1)S(1)} %pad_maximum_fusion.1), channel_id=1, source_target_pairs={{0,16},{4,20},{8,24},{12,28},{16,0},{20,4},{24,8},{28,12},{1,17},{... | collective-permute-start | bytes 2457608 | tf_op jit(solution)/shard_map/ppermute | solution.py:67
  44.4 17.1 %copy-start.5 = (bf16[1024,320]{0,1:T(8,128)(2,1)S(1)}, bf16[1024,320]{0,1:T(8,128)(2,1)}, u32[]{:S(2)}) copy-start(bf16[1024,320]{0,1:T(8,128)(2,1)} %param.9) | copy-start | bytes 1966084
  44.4 43.0 %copy-start.11 = (f32[1280]{0:T(1024)S(1)}, f32[1280]{0:T(1024)}, u32[]{:S(2)}) copy-start(f32[1280]{0:T(1024)} %param.12) | copy-start | bytes 15364
  44.4 40.3 %collective-permute-start.5 = (bf16[640,1280]{1,0:T(8,128)(2,1)S(1)}, bf16[640,1280]{1,0:T(8,128)(2,1)S(1)}, u32[]{:S(2)}, u32[]{:S(2)}) collective-permute-start(bf16[640,1280]{1,0:T(8,128)(2,1)S(1)} %pad_maximum_fusion.refs_2_), channel_id=1, source_target_pairs={{0,4},{4,0},{8,12},{12,8},{16,20},{20,16},{24,28},{28,24},{1,5},{5... | collective-permute-start | bytes 4915208 | tf_op jit(solution)/shard_map/ppermute | solution.py:70
  61.4 27.2 %collective-permute-start.2 = (bf16[640,1280]{1,0:T(8,128)(2,1)S(1)}, bf16[640,1280]{1,0:T(8,128)(2,1)}, u32[]{:S(2)}, u32[]{:S(2)}) collective-permute-start(bf16[640,1280]{1,0:T(8,128)(2,1)S(1)} %constant_dynamic-update-slice_fusion.refs_0_), channel_id=1, source_target_pairs={{0,4},{4,0},{8,12},{12,8},{16,20},{20,16},{24,28},{28,24},{1,5},{5... | collective-permute-start | bytes 4915208 | tf_op jit(solution)/shard_map/ppermute | solution.py:70
  61.5 19.1 %collective-permute-start.7 = (bf16[320,1024]{1,0:T(8,128)(2,1)S(1)}, bf16[320,1024]{1,0:T(8,128)(2,1)}, u32[]{:S(2)}, u32[]{:S(2)}) collective-permute-start(bf16[320,1024]{1,0:T(8,128)(2,1)S(1)} %bitcast.13), channel_id=1, source_target_pairs={{1,0},{2,1},{3,2},{5,4},{6,5},{7,6},{9,8},{10,9},{11,10},{13,12},{... | collective-permute-start | bytes 1966088 | tf_op jit(solution)/shard_map/ppermute | solution.py:30
  62.8 20.4 %collective-permute-start.6 = (bf16[320,1024]{1,0:T(8,128)(2,1)S(1)}, bf16[320,1024]{1,0:T(8,128)(2,1)}, u32[]{:S(2)}, u32[]{:S(2)}) collective-permute-start(bf16[320,1024]{1,0:T(8,128)(2,1)S(1)} %bitcast.14), channel_id=1, source_target_pairs={{0,1},{1,2},{2,3},{4,5},{5,6},{6,7},{8,9},{9,10},{10,11},{12,13},{... | collective-permute-start | bytes 1966088 | tf_op jit(solution)/shard_map/ppermute | solution.py:29
  80.6 19.1 %collective-permute-start.10 = (bf16[320,1024]{1,0:T(8,128)(2,1)}, bf16[320,1024]{1,0:T(8,128)(2,1)}, u32[]{:S(2)}, u32[]{:S(2)}) collective-permute-start(bf16[320,1024]{1,0:T(8,128)(2,1)} %collective-permute-done.7.refs_2_), channel_id=1, source_target_pairs={{1,0},{2,1},{5,4},{6,5},{9,8},{10,9},{13,12},{14,13},{17,16},{18,1... | collective-permute-start | bytes 1966088 | tf_op jit(solution)/shard_map/ppermute | solution.py:35
  81.9 31.9 %collective-permute-start.11 = (bf16[320,1024]{1,0:T(8,128)(2,1)}, bf16[320,1024]{1,0:T(8,128)(2,1)}, u32[]{:S(2)}, u32[]{:S(2)}) collective-permute-start(bf16[320,1024]{1,0:T(8,128)(2,1)} %collective-permute-done.7.refs_2_), channel_id=1, source_target_pairs={{2,0},{6,4},{10,8},{14,12},{18,16},{22,20},{26,24},{30,28}} | collective-permute-start | bytes 1966088 | tf_op jit(solution)/shard_map/ppermute | solution.py:35
  83.2 30.6 %collective-permute-start.8 = (bf16[320,1024]{1,0:T(8,128)(2,1)}, bf16[320,1024]{1,0:T(8,128)(2,1)}, u32[]{:S(2)}, u32[]{:S(2)}) collective-permute-start(bf16[320,1024]{1,0:T(8,128)(2,1)} %collective-permute-done.6.refs_1_), channel_id=1, source_target_pairs={{1,2},{2,3},{5,6},{6,7},{9,10},{10,11},{13,14},{14,15},{17,18},{18... | collective-permute-start | bytes 1966088 | tf_op jit(solution)/shard_map/ppermute | solution.py:34
  85.9 27.9 %collective-permute-start.9 = (bf16[320,1024]{1,0:T(8,128)(2,1)}, bf16[320,1024]{1,0:T(8,128)(2,1)}, u32[]{:S(2)}, u32[]{:S(2)}) collective-permute-start(bf16[320,1024]{1,0:T(8,128)(2,1)} %collective-permute-done.6.refs_1_), channel_id=1, source_target_pairs={{1,3},{5,7},{9,11},{13,15},{17,19},{21,23},{25,27},{29,31}} | collective-permute-start | bytes 1966088 | tf_op jit(solution)/shard_map/ppermute | solution.py:34
  90.1 23.7 %copy-start.2 = (f32[1280,1]{1,0:T(8,128)S(1)}, f32[1280,1]{1,0:T(8,128)}, u32[]{:S(2)}) copy-start(f32[1280,1]{1,0:T(8,128)} %reshape.18.gain) | copy-start | bytes 15364
  90.1 23.7 %copy-start.6 = (bf16[1024,320]{0,1:T(8,128)(2,1)S(1)}, bf16[1024,320]{0,1:T(8,128)(2,1)}, u32[]{:S(2)}) copy-start(bf16[1024,320]{0,1:T(8,128)(2,1)} %param.9) | copy-start | bytes 1966084
  124.2 24.7 %collective-permute-start.15 = (bf16[1280,128]{1,0:T(8,128)(2,1)S(1)}, bf16[1280,128]{1,0:T(8,128)(2,1)S(1)}, u32[]{:S(2)}, u32[]{:S(2)}) collective-permute-start(bf16[1280,128]{1,0:T(8,128)(2,1)S(1)} %get-tuple-element.20), channel_id=1, source_target_pairs={{2,1},{3,2},{6,5},{7,6},{10,9},{11,10},{14,13},{15,14},{18,17},{19... | collective-permute-start | bytes 983048 | tf_op jit(solution)/shard_map/ppermute | solution.py:57
  124.9 27.4 %collective-permute-start.16 = (bf16[1280,128]{1,0:T(8,128)(2,1)S(1)}, bf16[1280,128]{1,0:T(8,128)(2,1)S(1)}, u32[]{:S(2)}, u32[]{:S(2)}) collective-permute-start(bf16[1280,128]{1,0:T(8,128)(2,1)S(1)} %get-tuple-element.19), channel_id=1, source_target_pairs={{3,1},{7,5},{11,9},{15,13},{19,17},{23,21},{27,25},{31,29}} | collective-permute-start | bytes 983048 | tf_op jit(solution)/shard_map/ppermute | solution.py:57
  125.6 28.3 %collective-permute-start.12 = (bf16[1280,128]{1,0:T(8,128)(2,1)S(1)}, bf16[1280,128]{1,0:T(8,128)(2,1)S(1)}, u32[]{:S(2)}, u32[]{:S(2)}) collective-permute-start(bf16[1280,128]{1,0:T(8,128)(2,1)S(1)} %get-tuple-element.20), channel_id=1, source_target_pairs={{0,1},{1,2},{4,5},{5,6},{8,9},{9,10},{12,13},{13,14},{16,17},{17,1... | collective-permute-start | bytes 983048 | tf_op jit(solution)/shard_map/ppermute | solution.py:55
  143.7 22.4 %collective-permute-start.21 = (bf16[1280,128]{1,0:T(8,128)(2,1)S(1)}, bf16[1280,128]{1,0:T(8,128)(2,1)S(1)}, u32[]{:S(2)}, u32[]{:S(2)}) collective-permute-start(bf16[1280,128]{1,0:T(8,128)(2,1)S(1)} %get-tuple-element.25), channel_id=1, source_target_pairs={{2,1},{3,2},{6,5},{7,6},{10,9},{11,10},{14,13},{15,14},{18,17},{19... | collective-permute-start | bytes 983048 | tf_op jit(solution)/shard_map/ppermute | solution.py:57
  144.4 29.5 %collective-permute-start.18 = (bf16[1280,128]{1,0:T(8,128)(2,1)S(1)}, bf16[1280,128]{1,0:T(8,128)(2,1)S(1)}, u32[]{:S(2)}, u32[]{:S(2)}) collective-permute-start(bf16[1280,128]{1,0:T(8,128)(2,1)S(1)} %get-tuple-element.25), channel_id=1, source_target_pairs={{0,1},{1,2},{4,5},{5,6},{8,9},{9,10},{12,13},{13,14},{16,17},{17,1... | collective-permute-start | bytes 983048 | tf_op jit(solution)/shard_map/ppermute | solution.py:55
  148.9 15.1 %collective-permute-start.13 = (bf16[1280,128]{1,0:T(8,128)(2,1)S(1)}, bf16[1280,128]{1,0:T(8,128)(2,1)S(1)}, u32[]{:S(2)}, u32[]{:S(2)}) collective-permute-start(bf16[1280,128]{1,0:T(8,128)(2,1)S(1)} %get-tuple-element.21), channel_id=1, source_target_pairs={{0,2},{4,6},{8,10},{12,14},{16,18},{20,22},{24,26},{28,30}} | collective-permute-start | bytes 983048 | tf_op jit(solution)/shard_map/ppermute | solution.py:55
  152.3 19.3 %collective-permute-start.22 = (bf16[1280,128]{1,0:T(8,128)(2,1)S(1)}, bf16[1280,128]{1,0:T(8,128)(2,1)S(1)}, u32[]{:S(2)}, u32[]{:S(2)}) collective-permute-start(bf16[1280,128]{1,0:T(8,128)(2,1)S(1)} %get-tuple-element.24), channel_id=1, source_target_pairs={{3,1},{7,5},{11,9},{15,13},{19,17},{23,21},{27,25},{31,29}} | collective-permute-start | bytes 983048 | tf_op jit(solution)/shard_map/ppermute | solution.py:57
  153.9 20.1 %collective-permute-start.19 = (bf16[1280,128]{1,0:T(8,128)(2,1)S(1)}, bf16[1280,128]{1,0:T(8,128)(2,1)S(1)}, u32[]{:S(2)}, u32[]{:S(2)}) collective-permute-start(bf16[1280,128]{1,0:T(8,128)(2,1)S(1)} %get-tuple-element.26), channel_id=1, source_target_pairs={{0,2},{4,6},{8,10},{12,14},{16,18},{20,22},{24,26},{28,30}} | collective-permute-start | bytes 983048 | tf_op jit(solution)/shard_map/ppermute | solution.py:55
  164.1 16.6 %collective-permute-start.17 = (bf16[1280,128]{1,0:T(8,128)(2,1)}, bf16[1280,128]{1,0:T(8,128)(2,1)S(1)}, u32[]{:S(2)}, u32[]{:S(2)}) collective-permute-start(bf16[1280,128]{1,0:T(8,128)(2,1)} %add_convert_fusion.2), channel_id=1, source_target_pairs={{1,0},{2,1},{3,2},{5,4},{6,5},{7,6},{9,8},{10,9},{11,10},{13,12},{... | collective-permute-start | bytes 983048 | tf_op jit(solution)/shard_map/ppermute | solution.py:60
  166.2 13.9 %copy-start.9 = (bf16[1280,256]{1,0:T(8,128)(2,1)S(1)}, bf16[1280,256]{1,0:T(8,128)(2,1)}, u32[]{:S(2)}) copy-start(bf16[1280,256]{1,0:T(8,128)(2,1)} %param.14) | copy-start | bytes 1966084
  166.2 14.4 %collective-permute-start.14 = (bf16[1280,128]{1,0:T(8,128)(2,1)}, bf16[1280,128]{1,0:T(8,128)(2,1)}, u32[]{:S(2)}, u32[]{:S(2)}) collective-permute-start(bf16[1280,128]{1,0:T(8,128)(2,1)} %add_convert_fusion.3), channel_id=1, source_target_pairs={{0,1},{1,2},{2,3},{4,5},{5,6},{6,7},{8,9},{9,10},{10,11},{12,13},{... | collective-permute-start | bytes 983048 | tf_op jit(solution)/shard_map/ppermute | solution.py:59
  172.5 8.2 %copy-start.4 = (s32[32]{0:T(128)S(1)}, s32[32]{0:T(128)}, u32[]{:S(2)}) copy-start(s32[32]{0:T(128)} %widths.5) | copy-start | bytes 388
  172.5 13.6 %collective-permute-start.23 = (bf16[1280,128]{1,0:T(8,128)(2,1)}, bf16[1280,128]{1,0:T(8,128)(2,1)S(1)}, u32[]{:S(2)}, u32[]{:S(2)}) collective-permute-start(bf16[1280,128]{1,0:T(8,128)(2,1)} %add_convert_fusion), channel_id=1, source_target_pairs={{1,0},{2,1},{3,2},{5,4},{6,5},{7,6},{9,8},{10,9},{11,10},{13,12},{... | collective-permute-start | bytes 983048 | tf_op jit(solution)/shard_map/ppermute | solution.py:60
  174.8 11.3 %collective-permute-start.20 = (bf16[1280,128]{1,0:T(8,128)(2,1)}, bf16[1280,128]{1,0:T(8,128)(2,1)}, u32[]{:S(2)}, u32[]{:S(2)}) collective-permute-start(bf16[1280,128]{1,0:T(8,128)(2,1)} %add_convert_fusion.1), channel_id=1, source_target_pairs={{0,1},{1,2},{2,3},{4,5},{5,6},{6,7},{8,9},{9,10},{10,11},{12,13},{... | collective-permute-start | bytes 983048 | tf_op jit(solution)/shard_map/ppermute | solution.py:59
  (5 other events, 26.7 us)
where the time goes:
time: 233 us; the launch traced here: 232 us
  waiting for transfers between devices  93.6 us (40%)
  starting transfers between devices  52.1 us (22%)
  Pallas kernels  51.7 us (22%)
  blocking collectives  23.9 us (10%)
  other arithmetic  5.44 us (2%)
  local copies, waits for them, and re-layouts  4.36 us (2%)
    ppermute x4, waiting for transfers between devices, tm_gather(): got = lax.ppermute(x, 'tm', [(i, i ^ 1 << b) for i in range(size)])  52.6 us
    pallas_call x2, Pallas kernels, ffn(): pl.pallas_call(functools.partial(ffn_kernel, n, chunk, chunks), out_shape...  20.7 us
    ppermute x2, waiting for transfers between devices, line_gather(): l2.append(lax.ppermute(l1, 'chan', [(i, i - k) for i in range(k, n - 1)]))  19.6 us
    ppermute x4, starting transfers between devices, line_scatter(): lax.ppermute(parts[k], 'chan', [(i, i + k) for i in range(0, n - 1 - k)])  16.9 us
    all_gather x1, blocking collectives, compute(): near = lax.all_gather(state, 'chan')  14 us
    pallas_call x1, Pallas kernels, product(): pl.pallas_call(product_kernel, out_shape=jax.ShapeDtypeStruct((BAND, BAND...  13.8 us
    ppermute x1, waiting for transfers between devices, line_gather(): l1 = lax.ppermute(x, 'chan', [(i + 1, i) for i in range(n - 1)])  12.4 us
    pallas_call x2, Pallas kernels, tail(): pl.pallas_call(functools.partial(tail_kernel, first, last), out_shape=[ja...  11.8 us
  transfers between devices with their start and end apart: 24, of which 7 were waited for; matrix products, arithmetic and copies ran while one was open for 2% of the time, Pallas kernels for 9%

commit v1 on v0

--- a/solution.py
+++ b/solution.py
@@ -18,11 +18,18 @@
 NEG_SCORE = -1000000000.0
 CHUNKS = 2
 VMEM_LIMIT = 24 * 1024 * 1024
-FFN_VMEM = 40 * 1024 * 1024
+FFN_VMEM = 28 * 1024 * 1024
 
 
 f32 = jnp.float32
 bf16 = jnp.bfloat16
+
+
+def turn_gather(x, n):
+    got = [x]
+    for k in range(1, n):
+        got.append(lax.ppermute(x, "chan", [(i, (i + k) % n) for i in range(n)]))
+    return got
 
 
 def line_gather(x, n):
@@ -36,7 +43,9 @@
     return [x, r1, l1, *r2, *l2]
 
 
-def piece_at(a, z, n):
+def piece_at(a, z, n, straight):
+    if straight:
+        return (z - a) % n
     if a == z:
         return 0
     if a == z - 1:
@@ -52,12 +61,16 @@
     right = parts[0].astype(f32)
     left = parts[n - 2].astype(f32)
     for k in range(1, n - 1):
-        got = lax.ppermute(parts[k], "chan", [(i, i + k) for i in range(0, n - 1 - k)])
-        right = right + got.astype(f32)
-        got = lax.ppermute(parts[n - 2 - k], "chan", [(i, i - k) for i in range(k + 1, n)])
-        left = left + got.astype(f32)
-    from_left = lax.ppermute(right.astype(bf16), "chan", [(i, i + 1) for i in range(n - 1)])
-    from_right = lax.ppermute(left.astype(bf16), "chan", [(i + 1, i) for i in range(n - 1)])
+        to_right = lax.ppermute(parts[k], "chan", [(i, i + k) for i in range(0, n - 1 - k)])
+        to_left = lax.ppermute(
+            parts[n - 2 - k], "chan", [(i, i - k) for i in range(k + 1, n)]
+        )
+        right = right + to_right.astype(f32)
+        left = left + to_left.astype(f32)
+    right = right.astype(bf16)
+    left = left.astype(bf16)
+    from_left = lax.ppermute(right, "chan", [(i, i + 1) for i in range(n - 1)])
+    from_right = lax.ppermute(left, "chan", [(i + 1, i) for i in range(n - 1)])
     return from_left, from_right
 
 
@@ -71,9 +84,11 @@
     return x, got, dist
 
 
-def prepare_kernel(dist, meta, *refs):
+def prepare_kernel(dist, meta, gain, last_gain, ctc, *refs):
     ups, dns = refs[0:2], refs[2:4]
-    up_t, dn_t, up, usem, dsem = refs[4:]
+    up_t, dn_t, wide_gain, wide_last, ctc_t, up, usem, dsem = refs[4:]
+    wide_gain[...] = jnp.broadcast_to(gain[...], wide_gain.shape)
+    wide_last[...] = jnp.broadcast_to(last_gain[...], wide_last.shape)
     up_dist, dn_dist = dist
     tall = ups[0].shape[0] // len(up_dist)
     me = meta[1]
@@ -96,6 +111,8 @@
     dn_copies = copies(dns, dn_t, dsem, dn_dist)
     for c in up_copies + dn_copies:
         c.start()
+    for i in range(0, ctc.shape[0], 256):
+        ctc_t[:, i : i + 256] = ctc[i : i + 256, :].T
     for c in up_copies:
         c.wait()
     step = 256
@@ -107,7 +124,7 @@
         c.wait()
 
 
-def prepare(meta, ups, dns, dist, width):
+def prepare(meta, gain, last_gain, ctc, ups, dns, dist, width):
     hidden = ups[0].shape[1]
     count = 2 * len(dist[0])
     vmem = pl.BlockSpec(memory_space=pltpu.VMEM)
@@ -117,9 +134,12 @@
         out_shape=[
             jax.ShapeDtypeStruct((hidden, width), bf16),
             jax.ShapeDtypeStruct((width, hidden), bf16),
+            jax.ShapeDtypeStruct((width, LANES), f32),
+            jax.ShapeDtypeStruct((width, LANES), f32),
+            jax.ShapeDtypeStruct(ctc.shape[::-1], bf16),
         ],
-        in_specs=[pl.BlockSpec(memory_space=pltpu.SMEM)] + [anywhere] * 4,
-        out_specs=[vmem] * 2,
+        in_specs=[pl.BlockSpec(memory_space=pltpu.SMEM)] + [vmem] * 3 + [anywhere] * 4,
+        out_specs=[vmem] * 5,
         scratch_shapes=[
             pltpu.VMEM((width, hidden), bf16),
             pltpu.SemaphoreType.DMA((count,)),
@@ -130,14 +150,14 @@
             flops=0, bytes_accessed=8 * width * hidden, transcendentals=0
         ),
         name="prepare",
-    )(meta, *ups, *dns)
-
-
-def ffn_kernel(n, chunk, chunks, meta, gain, up_hbm, dn_hbm, *refs):
-    pieces = 1 + 2 + 2 * (n - 2)
+    )(meta, gain, last_gain, ctc, *ups, *dns)
+
+
+def ffn_kernel(n, straight, meta, gain, up_t, dn_t, *refs):
+    pieces = n if straight else 1 + 2 + 2 * (n - 2)
     xs = refs[:pieces]
     outs = refs[pieces : pieces + n]
-    xin, xn, hid, up_t, dn_t, terms, base, xsem, wsem, osem = refs[pieces + n :]
+    xin, xn, hid, terms, base, xsem, osem = refs[pieces + n :]
     width, rows = xin.shape
     feat = width // n
     fc = rows // n
@@ -148,30 +168,25 @@
             @pl.when(z == here)
             def _(a=a, here=here):
                 for r in range(n):
-                    column = (((here + r) % n) * chunks + chunk) * fc
+                    column = ((here + r) % n) * fc
                     pltpu.make_async_copy(
-                        xs[piece_at(a, here, n)].at[:, pl.ds(column, fc)],
+                        xs[piece_at(a, here, n, straight)].at[:, pl.ds(column, fc)],
                         xin.at[pl.ds(a * feat, feat), pl.ds(r * fc, fc)],
                         xsem.at[a * n + r],
                     ).start()
 
-    up_copy = pltpu.make_async_copy(up_hbm, up_t, wsem.at[0])
-    dn_copy = pltpu.make_async_copy(dn_hbm, dn_t, wsem.at[1])
-    up_copy.start()
-    dn_copy.start()
-
-    for r in range(n):
-        for a in range(n):
-            pltpu.make_async_copy(
-                xs[0].at[:, pl.ds(0, fc)],
-                xin.at[pl.ds(a * feat, feat), pl.ds(r * fc, fc)],
-                xsem.at[a * n + r],
-            ).wait()
-    up_copy.wait()
+
     hidden = up_t.shape[0]
     step = 256 if hidden % 256 == 0 else 128
-    half = max(rows // 2, 256)
+    half = 256
     for start in range(0, rows, half):
+        for r in range(start // fc, (start + half) // fc):
+            for a in range(n):
+                pltpu.make_async_copy(
+                    xs[0].at[:, pl.ds(0, fc)],
+                    xin.at[pl.ds(a * feat, feat), pl.ds(r * fc, fc)],
+                    xsem.at[a * n + r],
+                ).wait()
         for h in range(start, start + half, 128):
             x = xin[:, h : h + 128].astype(f32)
             mean = jnp.mean(x, axis=0, keepdims=True)
@@ -183,12 +198,16 @@
                 up_t[j : j + step, :], xn[:, start : start + half], preferred_element_type=f32
             )
             hid[j : j + step, start : start + half] = (a / (1.0 + jnp.exp(-a))).astype(bf16)
-    dn_copy.wait()
     copies = []
     for k, j in enumerate(range(0, width, 256)):
-        p = jnp.dot(dn_t[j : j + 256, :], hid[...], preferred_element_type=f32)
+        p = [
+            jnp.dot(
+                dn_t[j : j + 256, :], hid[:, start : start + 256], preferred_element_type=f32
+            )
+            for start in range(0, rows, 256)
+        ]
         for r in range(n):
-            term = p[:, r * fc : (r + 1) * fc]
+            term = p[r * fc // 256][:, r * fc % 256 :][:, :fc]
             if r == 0:
                 base[j : j + 256, :] = xin[j : j + 256, :fc].astype(f32) + 0.5 * term
                 src = base.at[pl.ds(j, 256)]
@@ -204,29 +223,25 @@
         copy.wait()
 
 
-def ffn(meta, gain, up_t, dn_t, xs, n, chunk, chunks):
+def ffn(meta, gain, up_t, dn_t, xs, n, straight):
     _, rows = xs[0].shape
-    rows = rows // chunks
     fc = rows // n
     hidden, width = up_t.shape
     vmem = pl.BlockSpec(memory_space=pltpu.VMEM)
     anywhere = pl.BlockSpec(memory_space=pl.ANY)
     return pl.pallas_call(
-        functools.partial(ffn_kernel, n, chunk, chunks),
+        functools.partial(ffn_kernel, n, straight),
         out_shape=[jax.ShapeDtypeStruct((width, fc), bf16)] * (n - 1)
         + [jax.ShapeDtypeStruct((width, fc), f32)],
-        in_specs=[pl.BlockSpec(memory_space=pltpu.SMEM), vmem] + [anywhere] * (2 + len(xs)),
+        in_specs=[pl.BlockSpec(memory_space=pltpu.SMEM)] + [vmem] * 3 + [anywhere] * len(xs),
         out_specs=[anywhere] * n,
         scratch_shapes=[
             pltpu.VMEM((width, rows), bf16),
             pltpu.VMEM((width, rows), bf16),
             pltpu.VMEM((hidden, rows), bf16),
-            pltpu.VMEM((hidden, width), bf16),
-            pltpu.VMEM((width, hidden), bf16),
             pltpu.VMEM((n - 1, width, fc), bf16),
             pltpu.VMEM((width, fc), f32),
             pltpu.SemaphoreType.DMA((n * n,)),
-            pltpu.SemaphoreType.DMA((2,)),
             pltpu.SemaphoreType.DMA((n * (width // 256),)),
         ],
         compiler_params=pltpu.CompilerParams(vmem_limit_bytes=FFN_VMEM),
@@ -248,18 +263,22 @@
 
 def tail_kernel(first, last, meta, starts, widths, base, left, right, gain, ctc_t, label_rows, *refs):
     if not first:
-        state_in, refs = refs[0], refs[1:]
+        emitted, state_in, refs = refs[0], refs[1], refs[2:]
     emit, state_out, gaps = refs
     start_in, width_in, start_out, width_out = band_states(meta[2], starts, widths)
 
     residual = base[...] + 0.5 * (left[...].astype(f32) + right[...].astype(f32))
     mean = jnp.mean(residual, axis=0, keepdims=True)
     var = jnp.mean(jnp.square(residual - mean), axis=0, keepdims=True)
-    normed = ((residual - mean) * lax.rsqrt(var + LN_EPSILON) * gain[...]).astype(bf16)
+    wide = jnp.concatenate([gain[...]] * (residual.shape[1] // LANES), axis=1)
+    normed = ((residual - mean) * lax.rsqrt(var + LN_EPSILON) * wide).astype(bf16)
     logits = jnp.dot(ctc_t[...], normed, preferred_element_type=f32)
     logits = logits - jnp.max(logits, axis=0, keepdims=True)
     emissions = (logits - jnp.log(jnp.sum(jnp.exp(logits), axis=0, keepdims=True))).T
-    emit[...] = emissions
+    before = emit.shape[0] - emissions.shape[0]
+    if before:
+        emit[:before, :] = emitted[...]
+    emit[before:, :] = emissions
 
     odd_start = lax.rem(start_in, 2)
     origin = start_in - odd_start
@@ -396,7 +415,10 @@
     shape = (BAND, BAND) if last else (RING * BAND // (8 * LANES), 8, LANES)
     return pl.pallas_call(
         functools.partial(tail_kernel, first, last),
-        out_shape=[jax.ShapeDtypeStruct((fc, vocab), f32), jax.ShapeDtypeStruct(shape, f32)],
+        out_shape=[
+            jax.ShapeDtypeStruct((fc + (0 if first else state[0].shape[0]), vocab), f32),
+            jax.ShapeDtypeStruct(shape, f32),
+        ],
         in_specs=[smem] * 3 + [vmem] * (6 + len(state)),
         out_specs=[vmem] * 2,
         scratch_shapes=[pltpu.VMEM((fc, LANES * PHASES // 2), f32)],
@@ -414,23 +436,14 @@
 
     def lap(k, _):
         left[...] = out[...]
-
-        def block(j, acc):
-            shift = lax.rem(BAND - 8 * j, BAND)
-            terms = [
-                pltpu.roll(left[8 * g : 8 * g + 8, :], shift, axis=1) for g in range(groups)
-            ]
-            later = mats[k, pl.ds(pl.multiple_of(8 * j, 8), 8), :]
-            acc = list(acc)
+        acc = [jnp.full((8, BAND), 64 * NEG_SCORE, f32) for _ in range(groups)]
+        for j in range(0, BAND, 8):
+            later = mats[k, j : j + 8, :]
             for u in range(8):
                 row = jnp.broadcast_to(later[u : u + 1], (8, BAND))
                 for g in range(groups):
-                    col = jnp.broadcast_to(terms[g][:, u : u + 1], (8, BAND))
-                    acc[g] = jnp.maximum(acc[g], col + row)
-            return tuple(acc)
-
-        none = jnp.full((8, BAND), 64 * NEG_SCORE, f32)
-        acc = lax.fori_loop(0, BAND // 8, block, (none,) * groups)
+                    col = left[8 * g : 8 * g + 8, j + u : j + u + 1]
+                    acc[g] = jnp.maximum(acc[g], jnp.broadcast_to(col, (8, BAND)) + row)
         for g in range(groups):
             out[8 * g : 8 * g + 8, :] = acc[g]
         return 0
@@ -498,25 +511,30 @@
     size = lax.axis_size("tm")
     me = lax.axis_index("tm")
     rows, feat = frames.shape
+    fd = rows // n
+    fc = fd // CHUNKS
     shard = me * n + z
     meta = jnp.stack([z, me, shard]).astype(jnp.int32)
     high = list(range(1, size.bit_length() - 1))
     label_rows = labels.reshape(-1, RING)
     gain = ffn_gain.reshape(-1, 1)
     last_gain = final_gain.reshape(-1, 1)
-    ctc_t = ctc_weight.T
-
-    gathered = line_gather(frames.T, n)
+
+    turned = frames.T
+    gathered = []
+    for c in range(CHUNKS):
+        cuts = [turned[:, (d * CHUNKS + c) * fc :][:, :fc] for d in range(n)]
+        cut = jnp.concatenate(cuts, axis=1)
+        gathered.append(turn_gather(cut, n) if c else line_gather(cut, n))
     up_own, up_other, dist = tm_gather(up_weight, size, high)
     dn_own, dn_other, dn_dist = tm_gather(down_weight.T, size, high[::-1])
-    up_t, dn_t = prepare(
-        meta, (up_own, up_other), (dn_own, dn_other), (dist, dn_dist), n * feat
+    up_t, dn_t, gain, last_gain, ctc_t = prepare(
+        meta, gain, last_gain, ctc_weight, (up_own, up_other), (dn_own, dn_other), (dist, dn_dist), n * feat
     )
 
-    state = ()
-    emitted = []
+    state = emissions = ()
     for c in range(CHUNKS):
-        *parts, base = ffn(meta, gain, up_t, dn_t, gathered, n, c, CHUNKS)
+        *parts, base = ffn(meta, gain, up_t, dn_t, gathered[c], n, c > 0)
         from_left, from_right = line_scatter(parts, n)
         emissions, state = tail(
             c == 0,
@@ -530,10 +548,8 @@
             last_gain,
             ctc_t,
             label_rows,
-            *((state,) if c else ()),
+            *((emissions, state) if c else ()),
         )
-        emitted.append(emissions)
-    emissions = jnp.concatenate(emitted, axis=0) if CHUNKS > 1 else emitted[0]
 
     near = lax.all_gather(state, "chan")
     far = lax.all_gather(product(near), "tm")

time: 233 us -> 194 us (0.83)
  waiting for transfers between devices: 93.6 us -> 54.2 us
  Pallas kernels: 51.7 us -> 43.5 us
  local copies, waits for them, and re-layouts: 4.36 us -> 8.31 us
  starting transfers between devices: 52.1 us -> 55.3 us
    ppermute x4, waiting for transfers between devices: 52.6 us -> 23.7 us  [tm_gather(): got = lax.ppermute(x, 'tm', [(i, i ^ 1 << b) for i in range(size)])]
    ppermute x1, waiting for transfers between devices: 12.4 us -> 2.15 us  [line_gather(): l1 = lax.ppermute(x, 'chan', [(i + 1, i) for i in range(n - 1)])]
    ppermute x4 -> x7, starting transfers between devices: 13.4 us -> 23.2 us  [the longest x3 10.7 us: turn_gather(): got.append(lax.ppermute(x, 'chan', [(i, (i + k) % n) for i in range(n)]))]
    ppermute x4, starting transfers between devices: 16.9 us -> 10.4 us  [line_scatter(): lax.ppermute(parts[k], 'chan', [(i, i + k) for i in range(0, n - 1 - k)])]
    pallas_call x1, Pallas kernels: 13.8 us -> 7.56 us  [product(): pl.pallas_call(product_kernel, out_shape=jax.ShapeDtypeStruct((BAND, BAND...]
    ppermute x2, waiting for transfers between devices: 19.6 us -> 14 us  [line_gather(): l2.append(lax.ppermute(l1, 'chan', [(i, i - k) for i in range(k, n - 1)]))]
    ppermute x1, waiting for transfers between devices: 0.01 us -> 5.45 us  [line_gather(): r1 = lax.ppermute(x, 'chan', [(i, i + 1) for i in range(n - 1)])]
    unnamed x29 -> x32, local copies, waits for them, and re-layouts: 2.95 us -> 6.13 us
  transfers between devices with their start and end apart: 24 -> 27, of which waited for: 7 -> 7; matrix products, arithmetic and copies ran while one was open for 2% -> 5% of each run, Pallas kernels for 9% -> 15%
where the time goes in v1:
time: 194 us; the launch traced here: 193 us
  starting transfers between devices  55.3 us (29%)
  waiting for transfers between devices  54.2 us (28%)
  Pallas kernels  43.5 us (22%)
  blocking collectives  24.7 us (13%)
  local copies, waits for them, and re-layouts  8.31 us (4%)
  other arithmetic  5.71 us (3%)
    ppermute x4, waiting for transfers between devices, tm_gather(): got = lax.ppermute(x, 'tm', [(i, i ^ 1 << b) for i in range(size)])  23.7 us
    pallas_call x2, Pallas kernels, ffn(): pl.pallas_call(functools.partial(ffn_kernel, n, straight), out_shape=[jax...  19.5 us
    all_gather x1, blocking collectives, compute(): near = lax.all_gather(state, 'chan')  14.9 us
    ppermute x2, waiting for transfers between devices, line_gather(): l2.append(lax.ppermute(l1, 'chan', [(i, i - k) for i in range(k, n - 1)]))  14 us
    pallas_call x2, Pallas kernels, tail(): pl.pallas_call(functools.partial(tail_kernel, first, last), out_shape=[ja...  11.3 us
    ppermute x3, starting transfers between devices, turn_gather(): got.append(lax.ppermute(x, 'chan', [(i, (i + k) % n) for i in range(n)]))  10.7 us
    ppermute x4, starting transfers between devices, line_scatter(): lax.ppermute(parts[k], 'chan', [(i, i + k) for i in range(0, n - 1 - k)])  10.4 us
    ppermute x2, starting transfers between devices, line_scatter(): from_left = lax.ppermute(right, 'chan', [(i, i + 1) for i in range(n - 1)])  10 us
  transfers between devices with their start and end apart: 27, of which 7 were waited for; matrix products, arithmetic and copies ran while one was open for 5% of the time, Pallas kernels for 15%

profile of v1, /device:TPU:0, one launch (start us, length us, event | category | flops | bytes accessed | tf_op | source)
XLA Modules:
  0.0 192.9 jit_solution(4362454040209086445)
XLA Ops:
  0.6 3.1 %collective-permute-start.3 = (bf16[160,1280]{1,0:T(8,128)(2,1)}, bf16[160,1280]{1,0:T(8,128)(2,1)S(1)}, u32[]{:S(2)}, u32[]{:S(2)}) collective-permute-start(bf16[160,1280]{1,0:T(8,128)(2,1)} %bitcast.10), channel_id=1, source_target_pairs={{0,16},{4,20},{8,24},{12,28},{16,0},{20,4},{24,8},{28,12},{1,17},{... | collective-permute-start | bytes 1228808 | tf_op jit(solution)/shard_map/ppermute | solution.py:80
  3.7 1.5 collective-permute-start
  5.2 8.2 %collective-permute-done.3 = bf16[160,1280]{1,0:T(8,128)(2,1)S(1)} collective-permute-done((bf16[160,1280]{1,0:T(8,128)(2,1)}, bf16[160,1280]{1,0:T(8,128)(2,1)S(1)}, u32[]{:S(2)}, u32[]{:S(2)}) %collective-permute-start.3) | collective-permute-done | bytes 409632 | tf_op jit(solution)/shard_map/ppermute | solution.py:80
  14.4 1.8 collective-permute-start.4
  16.3 1.6 collective-permute-start.1
  18.7 15.3 %collective-permute-done.4 = bf16[320,1280]{1,0:T(8,128)(2,1)S(1)} collective-permute-done((bf16[320,1280]{1,0:T(8,128)(2,1)S(1)}, bf16[320,1280]{1,0:T(8,128)(2,1)S(1)}, u32[]{:S(2)}, u32[]{:S(2)}) %collective-permute-start.4) | collective-permute-done | bytes 819232 | tf_op jit(solution)/shard_map/ppermute | solution.py:80
  37.2 4.2 %collective-permute-start.15 = (bf16[320,512]{1,0:T(8,128)(2,1)S(1)}, bf16[320,512]{1,0:T(8,128)(2,1)}, u32[]{:S(2)}, u32[]{:S(2)}) collective-permute-start(bf16[320,512]{1,0:T(8,128)(2,1)S(1)} %pad_maximum_fusion.4.refs_0_), channel_id=1, source_target_pairs={{0,1},{1,2},{2,3},{4,5},{5,6},{6,7},{8,9},{9,10},{10,11},{12,13},{... | collective-permute-start | bytes 983048 | tf_op jit(solution)/shard_map/ppermute | solution.py:36
  42.6 5.4 %collective-permute-done.15.refs_1_ = bf16[320,512]{1,0:T(8,128)(2,1)} collective-permute-done((bf16[320,512]{1,0:T(8,128)(2,1)S(1)}, bf16[320,512]{1,0:T(8,128)(2,1)}, u32[]{:S(2)}, u32[]{:S(2)}) %collective-permute-start.15) | collective-permute-done | bytes 327712 | tf_op jit(solution)/shard_map/ppermute | solution.py:36
  48.1 1.4 collective-permute-start.17
  49.5 1.4 collective-permute-start.18
  50.9 2.2 %collective-permute-done.16.refs_2_ = bf16[320,512]{1,0:T(8,128)(2,1)} collective-permute-done((bf16[320,512]{1,0:T(8,128)(2,1)S(1)}, bf16[320,512]{1,0:T(8,128)(2,1)}, u32[]{:S(2)}, u32[]{:S(2)}) %collective-permute-start.16) | collective-permute-done | bytes 327712 | tf_op jit(solution)/shard_map/ppermute | solution.py:37
  53.0 1.3 collective-permute-start.19
  58.3 4.9 %collective-permute-start.6 = (bf16[320,512]{1,0:T(8,128)(2,1)S(1)}, bf16[320,512]{1,0:T(8,128)(2,1)S(1)}, u32[]{:S(2)}, u32[]{:S(2)}) collective-permute-start(bf16[320,512]{1,0:T(8,128)(2,1)S(1)} %pad_maximum_fusion.3.refs_0_), channel_id=1, source_target_pairs={{0,1},{1,2},{2,3},{3,0},{4,5},{5,6},{6,7},{7,4},{8,9},{9,10},{10,1... | collective-permute-start | bytes 983048 | tf_op jit(solution)/shard_map/ppermute | solution.py:31
  63.2 1.4 copy-done.5
  65.7 3.9 %prepare.1 = (bf16[1280,1280]{1,0:T(8,128)(2,1)S(1)}, bf16[1280,1280]{1,0:T(8,128)(2,1)S(1)}, f32[1280,128]{1,0:T(8,128)S(1)}, f32[1280,128]{1,0:T(8,128)S(1)}, bf16[256,1280]{1,0:T(8,128)(2,1)S(1)}) custom-call(s32[3]{0:T(128)S(1)} %pad_add_fusion.meta, f32[1280,1]{1,0:T(8,128)S(1)} %reshape.18.gain, f32[1280,1]{1,0:T(8,128)S(1)} %reshape.19.last_gain, ...), custom_call_target="tpu_custom_call" | custom-call | bytes 13107200 | tf_op jit(solution)/shard_map/prepare/pallas_call | solution.py:132
  70.5 2.8 %collective-permute-start.7 = (bf16[320,512]{1,0:T(8,128)(2,1)S(1)}, bf16[320,512]{1,0:T(8,128)(2,1)S(1)}, u32[]{:S(2)}, u32[]{:S(2)}) collective-permute-start(bf16[320,512]{1,0:T(8,128)(2,1)S(1)} %pad_maximum_fusion.3.refs_0_), channel_id=1, source_target_pairs={{0,2},{1,3},{2,0},{3,1},{4,6},{5,7},{6,4},{7,5},{8,10},{9,11},{10,... | collective-permute-start | bytes 983048 | tf_op jit(solution)/shard_map/ppermute | solution.py:31
  73.3 2.9 %collective-permute-start.8 = (bf16[320,512]{1,0:T(8,128)(2,1)S(1)}, bf16[320,512]{1,0:T(8,128)(2,1)S(1)}, u32[]{:S(2)}, u32[]{:S(2)}) collective-permute-start(bf16[320,512]{1,0:T(8,128)(2,1)S(1)} %pad_maximum_fusion.3.refs_0_), channel_id=1, source_target_pairs={{0,3},{1,0},{2,1},{3,2},{4,7},{5,4},{6,5},{7,6},{8,11},{9,8},{10,9... | collective-permute-start | bytes 983048 | tf_op jit(solution)/shard_map/ppermute | solution.py:31
  76.2 14.0 %collective-permute-done.20.refs_6_ = bf16[320,512]{1,0:T(8,128)(2,1)} collective-permute-done((bf16[320,512]{1,0:T(8,128)(2,1)}, bf16[320,512]{1,0:T(8,128)(2,1)}, u32[]{:S(2)}, u32[]{:S(2)}) %collective-permute-start.20) | collective-permute-done | bytes 327712 | tf_op jit(solution)/shard_map/ppermute | solution.py:42
  90.3 10.4 %ffn.3 = (bf16[1280,128]{1,0:T(8,128)(2,1)S(1)}, bf16[1280,128]{1,0:T(8,128)(2,1)S(1)}, bf16[1280,128]{1,0:T(8,128)(2,1)S(1)}, f32[1280,128]{1,0:T(8,128)S(1)}) custom-call(s32[3]{0:T(128)S(1)} %pad_add_fusion.meta, f32[1280,128]{1,0:T(8,128)S(1)} %get-tuple-element.19.gain, bf16[1280,1280]{1,0:T(8,128)(2,1)S(1)} %get-tuple-element.20.up_t, ...), custom_call_target="tpu_custom_call" | custom-call | flops 3355443200 | bytes 10485760 | tf_op jit(solution)/shard_map/ffn/pallas_call | solution.py:232
  102.0 1.3 collective-permute-start.21
  103.4 9.1 %ffn.2 = (bf16[1280,128]{1,0:T(8,128)(2,1)S(1)}, bf16[1280,128]{1,0:T(8,128)(2,1)S(1)}, bf16[1280,128]{1,0:T(8,128)(2,1)S(1)}, f32[1280,128]{1,0:T(8,128)S(1)}) custom-call(s32[3]{0:T(128)S(1)} %pad_add_fusion.meta, f32[1280,128]{1,0:T(8,128)S(1)} %get-tuple-element.19.gain, bf16[1280,1280]{1,0:T(8,128)(2,1)S(1)} %get-tuple-element.20.up_t, ...), custom_call_target="tpu_custom_call" | custom-call | flops 3355443200 | bytes 10485760 | tf_op jit(solution)/shard_map/ffn/pallas_call | solution.py:232
  113.2 4.4 %collective-permute-start.9 = (bf16[1280,128]{1,0:T(8,128)(2,1)S(1)}, bf16[1280,128]{1,0:T(8,128)(2,1)S(1)}, u32[]{:S(2)}, u32[]{:S(2)}) collective-permute-start(bf16[1280,128]{1,0:T(8,128)(2,1)S(1)} %get-tuple-element.24), channel_id=1, source_target_pairs={{0,1},{1,2},{4,5},{5,6},{8,9},{9,10},{12,13},{13,14},{16,17},{17,1... | collective-permute-start | bytes 983048 | tf_op jit(solution)/shard_map/ppermute | solution.py:64
  117.7 3.4 %collective-permute-start.22 = (bf16[1280,128]{1,0:T(8,128)(2,1)S(1)}, bf16[1280,128]{1,0:T(8,128)(2,1)S(1)}, u32[]{:S(2)}, u32[]{:S(2)}) collective-permute-start(bf16[1280,128]{1,0:T(8,128)(2,1)S(1)} %get-tuple-element.31), channel_id=1, source_target_pairs={{0,2},{4,6},{8,10},{12,14},{16,18},{20,22},{24,26},{28,30}} | collective-permute-start | bytes 983048 | tf_op jit(solution)/shard_map/ppermute | solution.py:64
  122.6 1.3 collective-permute-start.10
  123.9 8.8 %collective-permute-done.22 = bf16[1280,128]{1,0:T(8,128)(2,1)S(1)} collective-permute-done((bf16[1280,128]{1,0:T(8,128)(2,1)S(1)}, bf16[1280,128]{1,0:T(8,128)(2,1)S(1)}, u32[]{:S(2)}, u32[]{:S(2)}) %collective-permute-start.22) | collective-permute-done | bytes 327712 | tf_op jit(solution)/shard_map/ppermute | solution.py:64
  134.9 5.4 %collective-permute-start.23 = (bf16[1280,128]{1,0:T(8,128)(2,1)}, bf16[1280,128]{1,0:T(8,128)(2,1)}, u32[]{:S(2)}, u32[]{:S(2)}) collective-permute-start(bf16[1280,128]{1,0:T(8,128)(2,1)} %add_convert_fusion.1), channel_id=1, source_target_pairs={{0,1},{1,2},{2,3},{4,5},{5,6},{6,7},{8,9},{9,10},{10,11},{12,13},{... | collective-permute-start | bytes 983048 | tf_op jit(solution)/shard_map/ppermute | solution.py:72
  143.4 4.6 %collective-permute-start.11 = (bf16[1280,128]{1,0:T(8,128)(2,1)}, bf16[1280,128]{1,0:T(8,128)(2,1)S(1)}, u32[]{:S(2)}, u32[]{:S(2)}) collective-permute-start(bf16[1280,128]{1,0:T(8,128)(2,1)} %add_convert_fusion.3), channel_id=1, source_target_pairs={{0,1},{1,2},{2,3},{4,5},{5,6},{6,7},{8,9},{9,10},{10,11},{12,13},{... | collective-permute-start | bytes 983048 | tf_op jit(solution)/shard_map/ppermute | solution.py:72
  148.0 5.5 %tail.2 = (f32[128,256]{1,0:T(8,128)S(1)}, f32[32,8,128]{2,1,0:T(8,128)S(1)}) custom-call(s32[3]{0:T(128)S(1)} %pad_add_fusion.meta, s32[32]{0:T(128)S(1)} %copy-done.7, s32[32]{0:T(128)S(1)} %copy-done.8, f32[1280,128]{1,0:T(8,128)S(1)} %get-tuple-element.28.base, bf16[1280,128]{1,0:T(8,128)(2,1)} %collective-permute-done.23.left, ...), custom_call_target="tpu_custom_call" | custom-call | flops 83886080 | bytes 2621440 | tf_op jit(solution)/shard_map/tail/pallas_call | solution.py:416
  153.5 5.8 %tail.3 = (f32[256,256]{1,0:T(8,128)}, f32[128,128]{1,0:T(8,128)S(1)}) custom-call(s32[3]{0:T(128)S(1)} %pad_add_fusion.meta, s32[32]{0:T(128)S(1)} %copy-done.7, s32[32]{0:T(128)S(1)} %copy-done.8, f32[1280,128]{1,0:T(8,128)S(1)} %get-tuple-element.22.base, bf16[1280,128]{1,0:T(8,128)(2,1)S(1)} %collective-permute-done.11.left, ...), custom_call_target="tpu_custom_call" | custom-call | flops 83886080 | bytes 2621440 | tf_op jit(solution)/shard_map/tail/pallas_call | solution.py:416
  159.4 14.9 %all-gather = f32[512,128]{1,0:T(8,128)S(1)} all-gather(f32[128,128]{1,0:T(8,128)S(1)} %get-tuple-element.35), channel_id=2, replica_groups=mesh['tm'=8,'chan'=4] {'chan'}, dimensions={0}, use_global_device_ids=true | all-gather | bytes 327680 | tf_op jit(solution)/shard_map/all_gather | solution.py:554
  174.4 7.6 %product.1 = f32[128,128]{1,0:T(8,128)S(1)} custom-call(f32[4,128,128]{2,1,0:T(8,128)S(1)} %bitcast.7), custom_call_target="tpu_custom_call" | custom-call | tf_op jit(solution)/shard_map/product/pallas_call | solution.py:456
  181.9 9.8 %all-gather.1 = f32[1024,128]{1,0:T(8,128)S(1)} all-gather(f32[128,128]{1,0:T(8,128)S(1)} %product.1), channel_id=3, replica_groups=mesh['tm'=8,'chan'=4] {'tm'}, dimensions={0}, use_global_device_ids=true | all-gather | bytes 589824 | tf_op jit(solution)/shard_map/all_gather | solution.py:555
  (78 shorter events, 22.3 us)
Async XLA Ops:
  0.6 15.6 %copy-start.10 = (bf16[160,1280]{1,0:T(8,128)(2,1)S(1)}, bf16[160,1280]{1,0:T(8,128)(2,1)}, u32[]{:S(2)}) copy-start(bf16[160,1280]{1,0:T(8,128)(2,1)} %param.10) | copy-start | bytes 1228804
  0.6 33.3 %copy-start.9 = (bf16[1280,160]{0,1:T(8,128)(2,1)S(1)}, bf16[1280,160]{0,1:T(8,128)(2,1)}, u32[]{:S(2)}) copy-start(bf16[1280,160]{0,1:T(8,128)(2,1)} %param.11) | copy-start | bytes 1228804
  0.6 12.7 %collective-permute-start.3 = (bf16[160,1280]{1,0:T(8,128)(2,1)}, bf16[160,1280]{1,0:T(8,128)(2,1)S(1)}, u32[]{:S(2)}, u32[]{:S(2)}) collective-permute-start(bf16[160,1280]{1,0:T(8,128)(2,1)} %bitcast.10), channel_id=1, source_target_pairs={{0,16},{4,20},{8,24},{12,28},{16,0},{20,4},{24,8},{28,12},{1,17},{... | collective-permute-start | bytes 1228808 | tf_op jit(solution)/shard_map/ppermute | solution.py:80
  3.7 12.5 %collective-permute-start = (bf16[160,1280]{1,0:T(8,128)(2,1)}, bf16[160,1280]{1,0:T(8,128)(2,1)S(1)}, u32[]{:S(2)}, u32[]{:S(2)}) collective-permute-start(bf16[160,1280]{1,0:T(8,128)(2,1)} %param.10), channel_id=1, source_target_pairs={{0,8},{4,12},{8,0},{12,4},{16,24},{20,28},{24,16},{28,20},{1,9},{5... | collective-permute-start | bytes 1228808 | tf_op jit(solution)/shard_map/ppermute | solution.py:80
  14.4 19.5 %collective-permute-start.4 = (bf16[320,1280]{1,0:T(8,128)(2,1)S(1)}, bf16[320,1280]{1,0:T(8,128)(2,1)S(1)}, u32[]{:S(2)}, u32[]{:S(2)}) collective-permute-start(bf16[320,1280]{1,0:T(8,128)(2,1)S(1)} %pad_maximum_fusion.2), channel_id=1, source_target_pairs={{0,8},{4,12},{8,0},{12,4},{16,24},{20,28},{24,16},{28,20},{1,9},{5... | collective-permute-start | bytes 2457608 | tf_op jit(solution)/shard_map/ppermute | solution.py:80
  16.3 18.9 %collective-permute-start.1 = (bf16[320,1280]{1,0:T(8,128)(2,1)S(1)}, bf16[320,1280]{1,0:T(8,128)(2,1)S(1)}, u32[]{:S(2)}, u32[]{:S(2)}) collective-permute-start(bf16[320,1280]{1,0:T(8,128)(2,1)S(1)} %pad_maximum_fusion.1), channel_id=1, source_target_pairs={{0,16},{4,20},{8,24},{12,28},{16,0},{20,4},{24,8},{28,12},{1,17},{... | collective-permute-start | bytes 2457608 | tf_op jit(solution)/shard_map/ppermute | solution.py:80
  34.0 20.3 %collective-permute-start.5 = (bf16[640,1280]{1,0:T(8,128)(2,1)S(1)}, bf16[640,1280]{1,0:T(8,128)(2,1)S(1)}, u32[]{:S(2)}, u32[]{:S(2)}) collective-permute-start(bf16[640,1280]{1,0:T(8,128)(2,1)S(1)} %pad_maximum_fusion.refs_2_), channel_id=1, source_target_pairs={{0,4},{4,0},{8,12},{12,8},{16,20},{20,16},{24,28},{28,24},{1,5},{5... | collective-permute-start | bytes 4915208 | tf_op jit(solution)/shard_map/ppermute | solution.py:83
  34.9 21.9 %copy-start.13 = (f32[1280]{0:T(1024)S(1)}, f32[1280]{0:T(1024)}, u32[]{:S(2)}) copy-start(f32[1280]{0:T(1024)} %param.12) | copy-start | bytes 15364
  36.2 20.8 %copy-start.14 = (f32[1280]{0:T(1024)S(1)}, f32[1280]{0:T(1024)}, u32[]{:S(2)}) copy-start(f32[1280]{0:T(1024)} %param.13) | copy-start | bytes 15364
  36.2 22.1 %collective-permute-start.2 = (bf16[640,1280]{1,0:T(8,128)(2,1)}, bf16[640,1280]{1,0:T(8,128)(2,1)}, u32[]{:S(2)}, u32[]{:S(2)}) collective-permute-start(bf16[640,1280]{1,0:T(8,128)(2,1)} %constant_dynamic-update-slice_fusion.refs_0_), channel_id=1, source_target_pairs={{0,4},{4,0},{8,12},{12,8},{16,20},{20,16},{24,28},{28,24},{1,5},{5... | collective-permute-start | bytes 4915208 | tf_op jit(solution)/shard_map/ppermute | solution.py:83
  37.2 10.9 %collective-permute-start.15 = (bf16[320,512]{1,0:T(8,128)(2,1)S(1)}, bf16[320,512]{1,0:T(8,128)(2,1)}, u32[]{:S(2)}, u32[]{:S(2)}) collective-permute-start(bf16[320,512]{1,0:T(8,128)(2,1)S(1)} %pad_maximum_fusion.4.refs_0_), channel_id=1, source_target_pairs={{0,1},{1,2},{2,3},{4,5},{5,6},{6,7},{8,9},{9,10},{10,11},{12,13},{... | collective-permute-start | bytes 983048 | tf_op jit(solution)/shard_map/ppermute | solution.py:36
  41.4 11.7 %collective-permute-start.16 = (bf16[320,512]{1,0:T(8,128)(2,1)S(1)}, bf16[320,512]{1,0:T(8,128)(2,1)}, u32[]{:S(2)}, u32[]{:S(2)}) collective-permute-start(bf16[320,512]{1,0:T(8,128)(2,1)S(1)} %pad_maximum_fusion.4.refs_0_), channel_id=1, source_target_pairs={{1,0},{2,1},{3,2},{5,4},{6,5},{7,6},{9,8},{10,9},{11,10},{13,12},{... | collective-permute-start | bytes 983048 | tf_op jit(solution)/shard_map/ppermute | solution.py:37
  48.1 22.4 %collective-permute-start.17 = (bf16[320,512]{1,0:T(8,128)(2,1)}, bf16[320,512]{1,0:T(8,128)(2,1)}, u32[]{:S(2)}, u32[]{:S(2)}) collective-permute-start(bf16[320,512]{1,0:T(8,128)(2,1)} %collective-permute-done.15.refs_1_), channel_id=1, source_target_pairs={{1,2},{2,3},{5,6},{6,7},{9,10},{10,11},{13,14},{14,15},{17,18},{18... | collective-permute-start | bytes 983048 | tf_op jit(solution)/shard_map/ppermute | solution.py:41
  49.5 23.8 %collective-permute-start.18 = (bf16[320,512]{1,0:T(8,128)(2,1)}, bf16[320,512]{1,0:T(8,128)(2,1)}, u32[]{:S(2)}, u32[]{:S(2)}) collective-permute-start(bf16[320,512]{1,0:T(8,128)(2,1)} %collective-permute-done.15.refs_1_), channel_id=1, source_target_pairs={{1,3},{5,7},{9,11},{13,15},{17,19},{21,23},{25,27},{29,31}} | collective-permute-start | bytes 983048 | tf_op jit(solution)/shard_map/ppermute | solution.py:41
  53.0 23.2 %collective-permute-start.19 = (bf16[320,512]{1,0:T(8,128)(2,1)}, bf16[320,512]{1,0:T(8,128)(2,1)}, u32[]{:S(2)}, u32[]{:S(2)}) collective-permute-start(bf16[320,512]{1,0:T(8,128)(2,1)} %collective-permute-done.16.refs_2_), channel_id=1, source_target_pairs={{1,0},{2,1},{5,4},{6,5},{9,8},{10,9},{13,12},{14,13},{17,16},{18,1... | collective-permute-start | bytes 983048 | tf_op jit(solution)/shard_map/ppermute | solution.py:42
  55.5 34.8 %collective-permute-start.20 = (bf16[320,512]{1,0:T(8,128)(2,1)}, bf16[320,512]{1,0:T(8,128)(2,1)}, u32[]{:S(2)}, u32[]{:S(2)}) collective-permute-start(bf16[320,512]{1,0:T(8,128)(2,1)} %collective-permute-done.16.refs_2_), channel_id=1, source_target_pairs={{2,0},{6,4},{10,8},{14,12},{18,16},{22,20},{26,24},{30,28}} | collective-permute-start | bytes 983048 | tf_op jit(solution)/shard_map/ppermute | solution.py:42
  58.3 43.7 %collective-permute-start.6 = (bf16[320,512]{1,0:T(8,128)(2,1)S(1)}, bf16[320,512]{1,0:T(8,128)(2,1)S(1)}, u32[]{:S(2)}, u32[]{:S(2)}) collective-permute-start(bf16[320,512]{1,0:T(8,128)(2,1)S(1)} %pad_maximum_fusion.3.refs_0_), channel_id=1, source_target_pairs={{0,1},{1,2},{2,3},{3,0},{4,5},{5,6},{6,7},{7,4},{8,9},{9,10},{10,1... | collective-permute-start | bytes 983048 | tf_op jit(solution)/shard_map/ppermute | solution.py:31
  70.5 30.2 %copy-start = (f32[1280,128]{1,0:T(8,128)}, f32[1280,128]{1,0:T(8,128)S(1)}, u32[]{:S(2)}) copy-start(f32[1280,128]{1,0:T(8,128)S(1)} %get-tuple-element.26.gain) | copy-start | bytes 1966084
  70.5 32.9 %collective-permute-start.7 = (bf16[320,512]{1,0:T(8,128)(2,1)S(1)}, bf16[320,512]{1,0:T(8,128)(2,1)S(1)}, u32[]{:S(2)}, u32[]{:S(2)}) collective-permute-start(bf16[320,512]{1,0:T(8,128)(2,1)S(1)} %pad_maximum_fusion.3.refs_0_), channel_id=1, source_target_pairs={{0,2},{1,3},{2,0},{3,1},{4,6},{5,7},{6,4},{7,5},{8,10},{9,11},{10,... | collective-permute-start | bytes 983048 | tf_op jit(solution)/shard_map/ppermute | solution.py:31
  73.3 30.1 %collective-permute-start.8 = (bf16[320,512]{1,0:T(8,128)(2,1)S(1)}, bf16[320,512]{1,0:T(8,128)(2,1)S(1)}, u32[]{:S(2)}, u32[]{:S(2)}) collective-permute-start(bf16[320,512]{1,0:T(8,128)(2,1)S(1)} %pad_maximum_fusion.3.refs_0_), channel_id=1, source_target_pairs={{0,3},{1,0},{2,1},{3,2},{4,7},{5,4},{6,5},{7,6},{8,11},{9,8},{10,9... | collective-permute-start | bytes 983048 | tf_op jit(solution)/shard_map/ppermute | solution.py:31
  100.6 17.0 %collective-permute-start.24 = (bf16[1280,128]{1,0:T(8,128)(2,1)S(1)}, bf16[1280,128]{1,0:T(8,128)(2,1)S(1)}, u32[]{:S(2)}, u32[]{:S(2)}) collective-permute-start(bf16[1280,128]{1,0:T(8,128)(2,1)S(1)} %get-tuple-element.30), channel_id=1, source_target_pairs={{2,1},{3,2},{6,5},{7,6},{10,9},{11,10},{14,13},{15,14},{18,17},{19... | collective-permute-start | bytes 983048 | tf_op jit(solution)/shard_map/ppermute | solution.py:65
  101.3 19.7 %collective-permute-start.25 = (bf16[1280,128]{1,0:T(8,128)(2,1)S(1)}, bf16[1280,128]{1,0:T(8,128)(2,1)S(1)}, u32[]{:S(2)}, u32[]{:S(2)}) collective-permute-start(bf16[1280,128]{1,0:T(8,128)(2,1)S(1)} %get-tuple-element.29), channel_id=1, source_target_pairs={{3,1},{7,5},{11,9},{15,13},{19,17},{23,21},{27,25},{31,29}} | collective-permute-start | bytes 983048 | tf_op jit(solution)/shard_map/ppermute | solution.py:65
  102.0 20.6 %collective-permute-start.21 = (bf16[1280,128]{1,0:T(8,128)(2,1)S(1)}, bf16[1280,128]{1,0:T(8,128)(2,1)S(1)}, u32[]{:S(2)}, u32[]{:S(2)}) collective-permute-start(bf16[1280,128]{1,0:T(8,128)(2,1)S(1)} %get-tuple-element.30), channel_id=1, source_target_pairs={{0,1},{1,2},{4,5},{5,6},{8,9},{9,10},{12,13},{13,14},{16,17},{17,1... | collective-permute-start | bytes 983048 | tf_op jit(solution)/shard_map/ppermute | solution.py:64
  112.5 22.4 %collective-permute-start.12 = (bf16[1280,128]{1,0:T(8,128)(2,1)S(1)}, bf16[1280,128]{1,0:T(8,128)(2,1)S(1)}, u32[]{:S(2)}, u32[]{:S(2)}) collective-permute-start(bf16[1280,128]{1,0:T(8,128)(2,1)S(1)} %get-tuple-element.24), channel_id=1, source_target_pairs={{2,1},{3,2},{6,5},{7,6},{10,9},{11,10},{14,13},{15,14},{18,17},{19... | collective-permute-start | bytes 983048 | tf_op jit(solution)/shard_map/ppermute | solution.py:65
  113.2 29.3 %collective-permute-start.9 = (bf16[1280,128]{1,0:T(8,128)(2,1)S(1)}, bf16[1280,128]{1,0:T(8,128)(2,1)S(1)}, u32[]{:S(2)}, u32[]{:S(2)}) collective-permute-start(bf16[1280,128]{1,0:T(8,128)(2,1)S(1)} %get-tuple-element.24), channel_id=1, source_target_pairs={{0,1},{1,2},{4,5},{5,6},{8,9},{9,10},{12,13},{13,14},{16,17},{17,1... | collective-permute-start | bytes 983048 | tf_op jit(solution)/shard_map/ppermute | solution.py:64
  117.7 15.1 %collective-permute-start.22 = (bf16[1280,128]{1,0:T(8,128)(2,1)S(1)}, bf16[1280,128]{1,0:T(8,128)(2,1)S(1)}, u32[]{:S(2)}, u32[]{:S(2)}) collective-permute-start(bf16[1280,128]{1,0:T(8,128)(2,1)S(1)} %get-tuple-element.31), channel_id=1, source_target_pairs={{0,2},{4,6},{8,10},{12,14},{16,18},{20,22},{24,26},{28,30}} | collective-permute-start | bytes 983048 | tf_op jit(solution)/shard_map/ppermute | solution.py:64
  121.1 19.3 %collective-permute-start.13 = (bf16[1280,128]{1,0:T(8,128)(2,1)S(1)}, bf16[1280,128]{1,0:T(8,128)(2,1)S(1)}, u32[]{:S(2)}, u32[]{:S(2)}) collective-permute-start(bf16[1280,128]{1,0:T(8,128)(2,1)S(1)} %get-tuple-element.23), channel_id=1, source_target_pairs={{3,1},{7,5},{11,9},{15,13},{19,17},{23,21},{27,25},{31,29}} | collective-permute-start | bytes 983048 | tf_op jit(solution)/shard_map/ppermute | solution.py:65
  122.6 19.9 %collective-permute-start.10 = (bf16[1280,128]{1,0:T(8,128)(2,1)S(1)}, bf16[1280,128]{1,0:T(8,128)(2,1)S(1)}, u32[]{:S(2)}, u32[]{:S(2)}) collective-permute-start(bf16[1280,128]{1,0:T(8,128)(2,1)S(1)} %get-tuple-element.25), channel_id=1, source_target_pairs={{0,2},{4,6},{8,10},{12,14},{16,18},{20,22},{24,26},{28,30}} | collective-permute-start | bytes 983048 | tf_op jit(solution)/shard_map/ppermute | solution.py:64
  132.7 15.2 %collective-permute-start.26 = (bf16[1280,128]{1,0:T(8,128)(2,1)}, bf16[1280,128]{1,0:T(8,128)(2,1)}, u32[]{:S(2)}, u32[]{:S(2)}) collective-permute-start(bf16[1280,128]{1,0:T(8,128)(2,1)} %add_convert_fusion), channel_id=1, source_target_pairs={{1,0},{2,1},{3,2},{5,4},{6,5},{7,6},{9,8},{10,9},{11,10},{13,12},{... | collective-permute-start | bytes 983048 | tf_op jit(solution)/shard_map/ppermute | solution.py:73
  134.9 13.1 %collective-permute-start.23 = (bf16[1280,128]{1,0:T(8,128)(2,1)}, bf16[1280,128]{1,0:T(8,128)(2,1)}, u32[]{:S(2)}, u32[]{:S(2)}) collective-permute-start(bf16[1280,128]{1,0:T(8,128)(2,1)} %add_convert_fusion.1), channel_id=1, source_target_pairs={{0,1},{1,2},{2,3},{4,5},{5,6},{6,7},{8,9},{9,10},{10,11},{12,13},{... | collective-permute-start | bytes 983048 | tf_op jit(solution)/shard_map/ppermute | solution.py:72
  141.2 12.3 %collective-permute-start.14 = (bf16[1280,128]{1,0:T(8,128)(2,1)}, bf16[1280,128]{1,0:T(8,128)(2,1)S(1)}, u32[]{:S(2)}, u32[]{:S(2)}) collective-permute-start(bf16[1280,128]{1,0:T(8,128)(2,1)} %add_convert_fusion.2), channel_id=1, source_target_pairs={{1,0},{2,1},{3,2},{5,4},{6,5},{7,6},{9,8},{10,9},{11,10},{13,12},{... | collective-permute-start | bytes 983048 | tf_op jit(solution)/shard_map/ppermute | solution.py:73
  143.4 10.1 %collective-permute-start.11 = (bf16[1280,128]{1,0:T(8,128)(2,1)}, bf16[1280,128]{1,0:T(8,128)(2,1)S(1)}, u32[]{:S(2)}, u32[]{:S(2)}) collective-permute-start(bf16[1280,128]{1,0:T(8,128)(2,1)} %add_convert_fusion.3), channel_id=1, source_target_pairs={{0,1},{1,2},{2,3},{4,5},{5,6},{6,7},{8,9},{9,10},{10,11},{12,13},{... | collective-permute-start | bytes 983048 | tf_op jit(solution)/shard_map/ppermute | solution.py:72
  (10 other events, 72.6 us)

commit v2 on v1

--- a/solution.py
+++ b/solution.py
@@ -430,8 +430,12 @@
     )(meta, starts, widths, base, left, right, gain, ctc_t, label_rows, *state)
 
 
-def product_kernel(mats, out, left):
+def product_kernel(n, meta, *refs):
+    got = refs[:n]
+    out, mats, left = refs[n:]
     groups = BAND // 8
+    for k in range(n):
+        mats[lax.rem(meta[0] + n - k, n)] = got[k][...]
     out[...] = mats[0]
 
     def lap(k, _):
@@ -448,20 +452,24 @@
             out[8 * g : 8 * g + 8, :] = acc[g]
         return 0
 
-    lax.fori_loop(1, mats.shape[0], lap, 0)
-
-
-def product(mats):
+    lax.fori_loop(1, n, lap, 0)
+
+
+def product(meta, got):
+    n = len(got)
     vmem = pl.BlockSpec(memory_space=pltpu.VMEM)
     return pl.pallas_call(
-        product_kernel,
-        out_shape=jax.ShapeDtypeStruct((BAND, BAND), f32),
-        in_specs=[vmem],
-        out_specs=vmem,
+        functools.partial(product_kernel, n),
+        out_shape=[
+            jax.ShapeDtypeStruct((BAND, BAND), f32),
+            jax.ShapeDtypeStruct((n, BAND, BAND), f32),
+        ],
+        in_specs=[pl.BlockSpec(memory_space=pltpu.SMEM)] + [vmem] * n,
+        out_specs=[vmem] * 2,
         scratch_shapes=[pltpu.VMEM((BAND, BAND), f32)],
         compiler_params=pltpu.CompilerParams(vmem_limit_bytes=VMEM_LIMIT),
         name="product",
-    )(mats)
+    )(meta, *got)
 
 
 def score_kernel(scale, meta, starts, widths, near, far, out):
@@ -551,8 +559,8 @@
             *((emissions, state) if c else ()),
         )
 
-    near = lax.all_gather(state, "chan")
-    far = lax.all_gather(product(near), "tm")
+    whole, near = product(meta, turn_gather(state, n))
+    far = lax.all_gather(whole, "tm")
     band_row = scores(1.0 / (rows * size), meta, starts, widths, near, far)
     return emissions, band_row
 

time: 194 us -> 189 us (0.974)
  blocking collectives: 24.7 us -> 9.85 us
  starting transfers between devices: 55.3 us -> 61.6 us
  waiting for transfers between devices: 54.2 us -> 57.7 us
    all_gather x2 -> x1, blocking collectives: 24.7 us -> 9.85 us  [compute(): far = lax.all_gather(whole, 'tm')]
    ppermute x3 -> x6, starting transfers between devices: 10.7 us -> 17 us  [turn_gather(): got.append(lax.ppermute(x, 'chan', [(i, (i + k) % n) for i in range(n)]))]
    ppermute x3 -> x6, waiting for transfers between devices: 0.01 us -> 3.45 us  [turn_gather(): got.append(lax.ppermute(x, 'chan', [(i, (i + k) % n) for i in range(n)]))]
  transfers between devices with their start and end apart: 27 -> 30, of which waited for: 7 -> 10; matrix products, arithmetic and copies ran while one was open for 5% -> 5% of each run, Pallas kernels for 15% -> 15%
where the time goes in v2:
time: 189 us; the launch traced here: 188 us
  starting transfers between devices  61.6 us (33%)
  waiting for transfers between devices  57.7 us (31%)
  Pallas kernels  44.1 us (23%)
  blocking collectives  9.85 us (5%)
  local copies, waits for them, and re-layouts  8.29 us (4%)
  other arithmetic  5.7 us (3%)
    ppermute x4, waiting for transfers between devices, tm_gather(): got = lax.ppermute(x, 'tm', [(i, i ^ 1 << b) for i in range(size)])  23.8 us
    pallas_call x2, Pallas kernels, ffn(): pl.pallas_call(functools.partial(ffn_kernel, n, straight), out_shape=[jax...  19.5 us
    ppermute x6, starting transfers between devices, turn_gather(): got.append(lax.ppermute(x, 'chan', [(i, (i + k) % n) for i in range(n)]))  17 us
    ppermute x2, waiting for transfers between devices, line_gather(): l2.append(lax.ppermute(l1, 'chan', [(i, i - k) for i in range(k, n - 1)]))  14 us
    pallas_call x2, Pallas kernels, tail(): pl.pallas_call(functools.partial(tail_kernel, first, last), out_shape=[ja...  11.3 us
    ppermute x4, starting transfers between devices, line_scatter(): lax.ppermute(parts[k], 'chan', [(i, i + k) for i in range(0, n - 1 - k)])  10.4 us
    ppermute x2, starting transfers between devices, line_scatter(): from_left = lax.ppermute(right, 'chan', [(i, i + 1) for i in range(n - 1)])  9.96 us
    all_gather x1, blocking collectives, compute(): far = lax.all_gather(whole, 'tm')  9.85 us
  transfers between devices with their start and end apart: 30, of which 10 were waited for; matrix products, arithmetic and copies ran while one was open for 5% of the time, Pallas kernels for 15%

profile of v2, /device:TPU:0, one launch (start us, length us, event | category | flops | bytes accessed | tf_op | source)
XLA Modules:
  0.0 188.4 jit_solution(244676795386807573)
XLA Ops:
  0.6 3.1 %collective-permute-start.3 = (bf16[160,1280]{1,0:T(8,128)(2,1)}, bf16[160,1280]{1,0:T(8,128)(2,1)S(1)}, u32[]{:S(2)}, u32[]{:S(2)}) collective-permute-start(bf16[160,1280]{1,0:T(8,128)(2,1)} %bitcast.7), channel_id=1, source_target_pairs={{0,16},{4,20},{8,24},{12,28},{16,0},{20,4},{24,8},{28,12},{1,17},{... | collective-permute-start | bytes 1228808 | tf_op jit(solution)/shard_map/ppermute | solution.py:80
  3.7 1.5 collective-permute-start
  5.2 8.2 %collective-permute-done.3 = bf16[160,1280]{1,0:T(8,128)(2,1)S(1)} collective-permute-done((bf16[160,1280]{1,0:T(8,128)(2,1)}, bf16[160,1280]{1,0:T(8,128)(2,1)S(1)}, u32[]{:S(2)}, u32[]{:S(2)}) %collective-permute-start.3) | collective-permute-done | bytes 409632 | tf_op jit(solution)/shard_map/ppermute | solution.py:80
  14.4 1.8 collective-permute-start.4
  16.3 1.6 collective-permute-start.1
  18.7 15.3 %collective-permute-done.4 = bf16[320,1280]{1,0:T(8,128)(2,1)S(1)} collective-permute-done((bf16[320,1280]{1,0:T(8,128)(2,1)S(1)}, bf16[320,1280]{1,0:T(8,128)(2,1)S(1)}, u32[]{:S(2)}, u32[]{:S(2)}) %collective-permute-start.4) | collective-permute-done | bytes 819232 | tf_op jit(solution)/shard_map/ppermute | solution.py:80
  37.2 4.2 %collective-permute-start.15 = (bf16[320,512]{1,0:T(8,128)(2,1)S(1)}, bf16[320,512]{1,0:T(8,128)(2,1)}, u32[]{:S(2)}, u32[]{:S(2)}) collective-permute-start(bf16[320,512]{1,0:T(8,128)(2,1)S(1)} %pad_maximum_fusion.4.refs_0_), channel_id=1, source_target_pairs={{0,1},{1,2},{2,3},{4,5},{5,6},{6,7},{8,9},{9,10},{10,11},{12,13},{... | collective-permute-start | bytes 983048 | tf_op jit(solution)/shard_map/ppermute | solution.py:36
  42.6 5.5 %collective-permute-done.15.refs_1_ = bf16[320,512]{1,0:T(8,128)(2,1)} collective-permute-done((bf16[320,512]{1,0:T(8,128)(2,1)S(1)}, bf16[320,512]{1,0:T(8,128)(2,1)}, u32[]{:S(2)}, u32[]{:S(2)}) %collective-permute-start.15) | collective-permute-done | bytes 327712 | tf_op jit(solution)/shard_map/ppermute | solution.py:36
  48.1 1.4 collective-permute-start.17
  49.5 1.4 collective-permute-start.18
  50.9 2.2 %collective-permute-done.16.refs_2_ = bf16[320,512]{1,0:T(8,128)(2,1)} collective-permute-done((bf16[320,512]{1,0:T(8,128)(2,1)S(1)}, bf16[320,512]{1,0:T(8,128)(2,1)}, u32[]{:S(2)}, u32[]{:S(2)}) %collective-permute-start.16) | collective-permute-done | bytes 327712 | tf_op jit(solution)/shard_map/ppermute | solution.py:37
  58.3 4.9 %collective-permute-start.6 = (bf16[320,512]{1,0:T(8,128)(2,1)S(1)}, bf16[320,512]{1,0:T(8,128)(2,1)S(1)}, u32[]{:S(2)}, u32[]{:S(2)}) collective-permute-start(bf16[320,512]{1,0:T(8,128)(2,1)S(1)} %pad_maximum_fusion.3.refs_0_), channel_id=1, source_target_pairs={{0,1},{1,2},{2,3},{3,0},{4,5},{5,6},{6,7},{7,4},{8,9},{9,10},{10,1... | collective-permute-start | bytes 983048 | tf_op jit(solution)/shard_map/ppermute | solution.py:31
  63.2 1.4 copy-done.5
  65.7 3.9 %prepare.1 = (bf16[1280,1280]{1,0:T(8,128)(2,1)S(1)}, bf16[1280,1280]{1,0:T(8,128)(2,1)S(1)}, f32[1280,128]{1,0:T(8,128)S(1)}, f32[1280,128]{1,0:T(8,128)S(1)}, bf16[256,1280]{1,0:T(8,128)(2,1)S(1)}) custom-call(s32[3]{0:T(128)S(1)} %pad_add_fusion.meta, f32[1280,1]{1,0:T(8,128)S(1)} %reshape.17.gain, f32[1280,1]{1,0:T(8,128)S(1)} %reshape.18.last_gain, ...), custom_call_target="tpu_custom_call" | custom-call | bytes 13107200 | tf_op jit(solution)/shard_map/prepare/pallas_call | solution.py:132
  70.5 2.8 %collective-permute-start.7 = (bf16[320,512]{1,0:T(8,128)(2,1)S(1)}, bf16[320,512]{1,0:T(8,128)(2,1)S(1)}, u32[]{:S(2)}, u32[]{:S(2)}) collective-permute-start(bf16[320,512]{1,0:T(8,128)(2,1)S(1)} %pad_maximum_fusion.3.refs_0_), channel_id=1, source_target_pairs={{0,2},{1,3},{2,0},{3,1},{4,6},{5,7},{6,4},{7,5},{8,10},{9,11},{10,... | collective-permute-start | bytes 983048 | tf_op jit(solution)/shard_map/ppermute | solution.py:31
  73.3 2.9 %collective-permute-start.8 = (bf16[320,512]{1,0:T(8,128)(2,1)S(1)}, bf16[320,512]{1,0:T(8,128)(2,1)S(1)}, u32[]{:S(2)}, u32[]{:S(2)}) collective-permute-start(bf16[320,512]{1,0:T(8,128)(2,1)S(1)} %pad_maximum_fusion.3.refs_0_), channel_id=1, source_target_pairs={{0,3},{1,0},{2,1},{3,2},{4,7},{5,4},{6,5},{7,6},{8,11},{9,8},{10,9... | collective-permute-start | bytes 983048 | tf_op jit(solution)/shard_map/ppermute | solution.py:31
  76.2 14.0 %collective-permute-done.20.refs_6_ = bf16[320,512]{1,0:T(8,128)(2,1)} collective-permute-done((bf16[320,512]{1,0:T(8,128)(2,1)}, bf16[320,512]{1,0:T(8,128)(2,1)}, u32[]{:S(2)}, u32[]{:S(2)}) %collective-permute-start.20) | collective-permute-done | bytes 327712 | tf_op jit(solution)/shard_map/ppermute | solution.py:42
  90.3 10.4 %ffn.3 = (bf16[1280,128]{1,0:T(8,128)(2,1)S(1)}, bf16[1280,128]{1,0:T(8,128)(2,1)S(1)}, bf16[1280,128]{1,0:T(8,128)(2,1)S(1)}, f32[1280,128]{1,0:T(8,128)S(1)}) custom-call(s32[3]{0:T(128)S(1)} %pad_add_fusion.meta, f32[1280,128]{1,0:T(8,128)S(1)} %get-tuple-element.21.gain, bf16[1280,1280]{1,0:T(8,128)(2,1)S(1)} %get-tuple-element.22.up_t, ...), custom_call_target="tpu_custom_call" | custom-call | flops 3355443200 | bytes 10485760 | tf_op jit(solution)/shard_map/ffn/pallas_call | solution.py:232
  102.0 1.3 collective-permute-start.21
  103.4 9.1 %ffn.2 = (bf16[1280,128]{1,0:T(8,128)(2,1)S(1)}, bf16[1280,128]{1,0:T(8,128)(2,1)S(1)}, bf16[1280,128]{1,0:T(8,128)(2,1)S(1)}, f32[1280,128]{1,0:T(8,128)S(1)}) custom-call(s32[3]{0:T(128)S(1)} %pad_add_fusion.meta, f32[1280,128]{1,0:T(8,128)S(1)} %get-tuple-element.21.gain, bf16[1280,1280]{1,0:T(8,128)(2,1)S(1)} %get-tuple-element.22.up_t, ...), custom_call_target="tpu_custom_call" | custom-call | flops 3355443200 | bytes 10485760 | tf_op jit(solution)/shard_map/ffn/pallas_call | solution.py:232
  113.2 4.4 %collective-permute-start.9 = (bf16[1280,128]{1,0:T(8,128)(2,1)S(1)}, bf16[1280,128]{1,0:T(8,128)(2,1)S(1)}, u32[]{:S(2)}, u32[]{:S(2)}) collective-permute-start(bf16[1280,128]{1,0:T(8,128)(2,1)S(1)} %get-tuple-element.26), channel_id=1, source_target_pairs={{0,1},{1,2},{4,5},{5,6},{8,9},{9,10},{12,13},{13,14},{16,17},{17,1... | collective-permute-start | bytes 983048 | tf_op jit(solution)/shard_map/ppermute | solution.py:64
  117.7 3.4 %collective-permute-start.22 = (bf16[1280,128]{1,0:T(8,128)(2,1)S(1)}, bf16[1280,128]{1,0:T(8,128)(2,1)S(1)}, u32[]{:S(2)}, u32[]{:S(2)}) collective-permute-start(bf16[1280,128]{1,0:T(8,128)(2,1)S(1)} %get-tuple-element.33), channel_id=1, source_target_pairs={{0,2},{4,6},{8,10},{12,14},{16,18},{20,22},{24,26},{28,30}} | collective-permute-start | bytes 983048 | tf_op jit(solution)/shard_map/ppermute | solution.py:64
  123.9 8.8 %collective-permute-done.22 = bf16[1280,128]{1,0:T(8,128)(2,1)S(1)} collective-permute-done((bf16[1280,128]{1,0:T(8,128)(2,1)S(1)}, bf16[1280,128]{1,0:T(8,128)(2,1)S(1)}, u32[]{:S(2)}, u32[]{:S(2)}) %collective-permute-start.22) | collective-permute-done | bytes 327712 | tf_op jit(solution)/shard_map/ppermute | solution.py:64
  134.9 5.4 %collective-permute-start.23 = (bf16[1280,128]{1,0:T(8,128)(2,1)}, bf16[1280,128]{1,0:T(8,128)(2,1)}, u32[]{:S(2)}, u32[]{:S(2)}) collective-permute-start(bf16[1280,128]{1,0:T(8,128)(2,1)} %add_convert_fusion.1), channel_id=1, source_target_pairs={{0,1},{1,2},{2,3},{4,5},{5,6},{6,7},{8,9},{9,10},{10,11},{12,13},{... | collective-permute-start | bytes 983048 | tf_op jit(solution)/shard_map/ppermute | solution.py:72
  143.4 4.6 %collective-permute-start.11 = (bf16[1280,128]{1,0:T(8,128)(2,1)}, bf16[1280,128]{1,0:T(8,128)(2,1)S(1)}, u32[]{:S(2)}, u32[]{:S(2)}) collective-permute-start(bf16[1280,128]{1,0:T(8,128)(2,1)} %add_convert_fusion.3), channel_id=1, source_target_pairs={{0,1},{1,2},{2,3},{4,5},{5,6},{6,7},{8,9},{9,10},{10,11},{12,13},{... | collective-permute-start | bytes 983048 | tf_op jit(solution)/shard_map/ppermute | solution.py:72
  148.0 5.5 %tail.2 = (f32[128,256]{1,0:T(8,128)S(1)}, f32[32,8,128]{2,1,0:T(8,128)S(1)}) custom-call(s32[3]{0:T(128)S(1)} %pad_add_fusion.meta, s32[32]{0:T(128)S(1)} %copy-done.7, s32[32]{0:T(128)S(1)} %copy-done.8, f32[1280,128]{1,0:T(8,128)S(1)} %get-tuple-element.30.base, bf16[1280,128]{1,0:T(8,128)(2,1)} %collective-permute-done.23.left, ...), custom_call_target="tpu_custom_call" | custom-call | flops 83886080 | bytes 2621440 | tf_op jit(solution)/shard_map/tail/pallas_call | solution.py:416
  153.5 5.9 %tail.3 = (f32[256,256]{1,0:T(8,128)}, f32[128,128]{1,0:T(8,128)S(1)}) custom-call(s32[3]{0:T(128)S(1)} %pad_add_fusion.meta, s32[32]{0:T(128)S(1)} %copy-done.7, s32[32]{0:T(128)S(1)} %copy-done.8, f32[1280,128]{1,0:T(8,128)S(1)} %get-tuple-element.24.base, bf16[1280,128]{1,0:T(8,128)(2,1)S(1)} %collective-permute-done.11.left, ...), custom_call_target="tpu_custom_call" | custom-call | flops 83886080 | bytes 2621440 | tf_op jit(solution)/shard_map/tail/pallas_call | solution.py:416
  159.4 2.0 %collective-permute-start.27 = (f32[128,128]{1,0:T(8,128)S(1)}, f32[128,128]{1,0:T(8,128)S(1)}, u32[]{:S(2)}, u32[]{:S(2)}) collective-permute-start(f32[128,128]{1,0:T(8,128)S(1)} %get-tuple-element.37.refs_0_), channel_id=1, source_target_pairs={{0,1},{1,2},{2,3},{3,0},{4,5},{5,6},{6,7},{7,4},{8,9},{9,10},{10,1... | collective-permute-start | bytes 196616 | tf_op jit(solution)/shard_map/ppermute | solution.py:31
  161.4 3.6 %collective-permute-start.28 = (f32[128,128]{1,0:T(8,128)S(1)}, f32[128,128]{1,0:T(8,128)S(1)}, u32[]{:S(2)}, u32[]{:S(2)}) collective-permute-start(f32[128,128]{1,0:T(8,128)S(1)} %get-tuple-element.37.refs_0_), channel_id=1, source_target_pairs={{0,2},{1,3},{2,0},{3,1},{4,6},{5,7},{6,4},{7,5},{8,10},{9,11},{10,... | collective-permute-start | bytes 196616 | tf_op jit(solution)/shard_map/ppermute | solution.py:31
  167.3 1.9 collective-permute-done.29.refs_3_
  169.2 8.1 %product.1 = (f32[128,128]{1,0:T(8,128)S(1)}, f32[4,128,128]{2,1,0:T(8,128)S(1)}) custom-call(s32[3]{0:T(128)S(1)} %pad_add_fusion.meta, f32[128,128]{1,0:T(8,128)S(1)} %get-tuple-element.37.refs_0_, f32[128,128]{1,0:T(8,128)S(1)} %collective-permute-done.27.refs_1_, f32[128,128]{1,0:T(8,128)S(1)} %collective-permute-done.28.refs_2_, ...), custom_call_target="tpu_custom_call" | custom-call | tf_op jit(solution)/shard_map/product/pallas_call | solution.py:461
  177.3 9.9 %all-gather = f32[1024,128]{1,0:T(8,128)S(1)} all-gather(f32[128,128]{1,0:T(8,128)S(1)} %get-tuple-element.39), channel_id=2, replica_groups=mesh['tm'=8,'chan'=4] {'tm'}, dimensions={0}, use_global_device_ids=true | all-gather | bytes 589824 | tf_op jit(solution)/shard_map/all_gather | solution.py:563
  (83 shorter events, 27.2 us)
Async XLA Ops:
  0.6 33.3 %copy-start.9 = (bf16[1280,160]{0,1:T(8,128)(2,1)S(1)}, bf16[1280,160]{0,1:T(8,128)(2,1)}, u32[]{:S(2)}) copy-start(bf16[1280,160]{0,1:T(8,128)(2,1)} %param.11) | copy-start | bytes 1228804
  0.6 12.7 %collective-permute-start.3 = (bf16[160,1280]{1,0:T(8,128)(2,1)}, bf16[160,1280]{1,0:T(8,128)(2,1)S(1)}, u32[]{:S(2)}, u32[]{:S(2)}) collective-permute-start(bf16[160,1280]{1,0:T(8,128)(2,1)} %bitcast.7), channel_id=1, source_target_pairs={{0,16},{4,20},{8,24},{12,28},{16,0},{20,4},{24,8},{28,12},{1,17},{... | collective-permute-start | bytes 1228808 | tf_op jit(solution)/shard_map/ppermute | solution.py:80
  3.7 12.5 %collective-permute-start = (bf16[160,1280]{1,0:T(8,128)(2,1)}, bf16[160,1280]{1,0:T(8,128)(2,1)S(1)}, u32[]{:S(2)}, u32[]{:S(2)}) collective-permute-start(bf16[160,1280]{1,0:T(8,128)(2,1)} %param.10), channel_id=1, source_target_pairs={{0,8},{4,12},{8,0},{12,4},{16,24},{20,28},{24,16},{28,20},{1,9},{5... | collective-permute-start | bytes 1228808 | tf_op jit(solution)/shard_map/ppermute | solution.py:80
  14.4 19.5 %collective-permute-start.4 = (bf16[320,1280]{1,0:T(8,128)(2,1)S(1)}, bf16[320,1280]{1,0:T(8,128)(2,1)S(1)}, u32[]{:S(2)}, u32[]{:S(2)}) collective-permute-start(bf16[320,1280]{1,0:T(8,128)(2,1)S(1)} %pad_maximum_fusion.2), channel_id=1, source_target_pairs={{0,8},{4,12},{8,0},{12,4},{16,24},{20,28},{24,16},{28,20},{1,9},{5... | collective-permute-start | bytes 2457608 | tf_op jit(solution)/shard_map/ppermute | solution.py:80
  16.3 18.9 %collective-permute-start.1 = (bf16[320,1280]{1,0:T(8,128)(2,1)S(1)}, bf16[320,1280]{1,0:T(8,128)(2,1)S(1)}, u32[]{:S(2)}, u32[]{:S(2)}) collective-permute-start(bf16[320,1280]{1,0:T(8,128)(2,1)S(1)} %pad_maximum_fusion.1), channel_id=1, source_target_pairs={{0,16},{4,20},{8,24},{12,28},{16,0},{20,4},{24,8},{28,12},{1,17},{... | collective-permute-start | bytes 2457608 | tf_op jit(solution)/shard_map/ppermute | solution.py:80
  34.0 20.3 %collective-permute-start.5 = (bf16[640,1280]{1,0:T(8,128)(2,1)S(1)}, bf16[640,1280]{1,0:T(8,128)(2,1)S(1)}, u32[]{:S(2)}, u32[]{:S(2)}) collective-permute-start(bf16[640,1280]{1,0:T(8,128)(2,1)S(1)} %pad_maximum_fusion.refs_2_), channel_id=1, source_target_pairs={{0,4},{4,0},{8,12},{12,8},{16,20},{20,16},{24,28},{28,24},{1,5},{5... | collective-permute-start | bytes 4915208 | tf_op jit(solution)/shard_map/ppermute | solution.py:83
  36.2 22.1 %collective-permute-start.2 = (bf16[640,1280]{1,0:T(8,128)(2,1)}, bf16[640,1280]{1,0:T(8,128)(2,1)}, u32[]{:S(2)}, u32[]{:S(2)}) collective-permute-start(bf16[640,1280]{1,0:T(8,128)(2,1)} %constant_dynamic-update-slice_fusion.refs_0_), channel_id=1, source_target_pairs={{0,4},{4,0},{8,12},{12,8},{16,20},{20,16},{24,28},{28,24},{1,5},{5... | collective-permute-start | bytes 4915208 | tf_op jit(solution)/shard_map/ppermute | solution.py:83
  37.2 10.9 %collective-permute-start.15 = (bf16[320,512]{1,0:T(8,128)(2,1)S(1)}, bf16[320,512]{1,0:T(8,128)(2,1)}, u32[]{:S(2)}, u32[]{:S(2)}) collective-permute-start(bf16[320,512]{1,0:T(8,128)(2,1)S(1)} %pad_maximum_fusion.4.refs_0_), channel_id=1, source_target_pairs={{0,1},{1,2},{2,3},{4,5},{5,6},{6,7},{8,9},{9,10},{10,11},{12,13},{... | collective-permute-start | bytes 983048 | tf_op jit(solution)/shard_map/ppermute | solution.py:36
  41.3 11.7 %collective-permute-start.16 = (bf16[320,512]{1,0:T(8,128)(2,1)S(1)}, bf16[320,512]{1,0:T(8,128)(2,1)}, u32[]{:S(2)}, u32[]{:S(2)}) collective-permute-start(bf16[320,512]{1,0:T(8,128)(2,1)S(1)} %pad_maximum_fusion.4.refs_0_), channel_id=1, source_target_pairs={{1,0},{2,1},{3,2},{5,4},{6,5},{7,6},{9,8},{10,9},{11,10},{13,12},{... | collective-permute-start | bytes 983048 | tf_op jit(solution)/shard_map/ppermute | solution.py:37
  48.1 22.4 %collective-permute-start.17 = (bf16[320,512]{1,0:T(8,128)(2,1)}, bf16[320,512]{1,0:T(8,128)(2,1)}, u32[]{:S(2)}, u32[]{:S(2)}) collective-permute-start(bf16[320,512]{1,0:T(8,128)(2,1)} %collective-permute-done.15.refs_1_), channel_id=1, source_target_pairs={{1,2},{2,3},{5,6},{6,7},{9,10},{10,11},{13,14},{14,15},{17,18},{18... | collective-permute-start | bytes 983048 | tf_op jit(solution)/shard_map/ppermute | solution.py:41
  49.5 23.9 %collective-permute-start.18 = (bf16[320,512]{1,0:T(8,128)(2,1)}, bf16[320,512]{1,0:T(8,128)(2,1)}, u32[]{:S(2)}, u32[]{:S(2)}) collective-permute-start(bf16[320,512]{1,0:T(8,128)(2,1)} %collective-permute-done.15.refs_1_), channel_id=1, source_target_pairs={{1,3},{5,7},{9,11},{13,15},{17,19},{21,23},{25,27},{29,31}} | collective-permute-start | bytes 983048 | tf_op jit(solution)/shard_map/ppermute | solution.py:41
  53.0 23.2 %collective-permute-start.19 = (bf16[320,512]{1,0:T(8,128)(2,1)}, bf16[320,512]{1,0:T(8,128)(2,1)}, u32[]{:S(2)}, u32[]{:S(2)}) collective-permute-start(bf16[320,512]{1,0:T(8,128)(2,1)} %collective-permute-done.16.refs_2_), channel_id=1, source_target_pairs={{1,0},{2,1},{5,4},{6,5},{9,8},{10,9},{13,12},{14,13},{17,16},{18,1... | collective-permute-start | bytes 983048 | tf_op jit(solution)/shard_map/ppermute | solution.py:42
  55.5 34.8 %collective-permute-start.20 = (bf16[320,512]{1,0:T(8,128)(2,1)}, bf16[320,512]{1,0:T(8,128)(2,1)}, u32[]{:S(2)}, u32[]{:S(2)}) collective-permute-start(bf16[320,512]{1,0:T(8,128)(2,1)} %collective-permute-done.16.refs_2_), channel_id=1, source_target_pairs={{2,0},{6,4},{10,8},{14,12},{18,16},{22,20},{26,24},{30,28}} | collective-permute-start | bytes 983048 | tf_op jit(solution)/shard_map/ppermute | solution.py:42
  58.3 43.7 %collective-permute-start.6 = (bf16[320,512]{1,0:T(8,128)(2,1)S(1)}, bf16[320,512]{1,0:T(8,128)(2,1)S(1)}, u32[]{:S(2)}, u32[]{:S(2)}) collective-permute-start(bf16[320,512]{1,0:T(8,128)(2,1)S(1)} %pad_maximum_fusion.3.refs_0_), channel_id=1, source_target_pairs={{0,1},{1,2},{2,3},{3,0},{4,5},{5,6},{6,7},{7,4},{8,9},{9,10},{10,1... | collective-permute-start | bytes 983048 | tf_op jit(solution)/shard_map/ppermute | solution.py:31
  70.5 30.2 %copy-start = (f32[1280,128]{1,0:T(8,128)}, f32[1280,128]{1,0:T(8,128)S(1)}, u32[]{:S(2)}) copy-start(f32[1280,128]{1,0:T(8,128)S(1)} %get-tuple-element.28.gain) | copy-start | bytes 1966084
  70.5 32.9 %collective-permute-start.7 = (bf16[320,512]{1,0:T(8,128)(2,1)S(1)}, bf16[320,512]{1,0:T(8,128)(2,1)S(1)}, u32[]{:S(2)}, u32[]{:S(2)}) collective-permute-start(bf16[320,512]{1,0:T(8,128)(2,1)S(1)} %pad_maximum_fusion.3.refs_0_), channel_id=1, source_target_pairs={{0,2},{1,3},{2,0},{3,1},{4,6},{5,7},{6,4},{7,5},{8,10},{9,11},{10,... | collective-permute-start | bytes 983048 | tf_op jit(solution)/shard_map/ppermute | solution.py:31
  73.3 30.1 %collective-permute-start.8 = (bf16[320,512]{1,0:T(8,128)(2,1)S(1)}, bf16[320,512]{1,0:T(8,128)(2,1)S(1)}, u32[]{:S(2)}, u32[]{:S(2)}) collective-permute-start(bf16[320,512]{1,0:T(8,128)(2,1)S(1)} %pad_maximum_fusion.3.refs_0_), channel_id=1, source_target_pairs={{0,3},{1,0},{2,1},{3,2},{4,7},{5,4},{6,5},{7,6},{8,11},{9,8},{10,9... | collective-permute-start | bytes 983048 | tf_op jit(solution)/shard_map/ppermute | solution.py:31
  100.7 17.0 %collective-permute-start.24 = (bf16[1280,128]{1,0:T(8,128)(2,1)S(1)}, bf16[1280,128]{1,0:T(8,128)(2,1)S(1)}, u32[]{:S(2)}, u32[]{:S(2)}) collective-permute-start(bf16[1280,128]{1,0:T(8,128)(2,1)S(1)} %get-tuple-element.32), channel_id=1, source_target_pairs={{2,1},{3,2},{6,5},{7,6},{10,9},{11,10},{14,13},{15,14},{18,17},{19... | collective-permute-start | bytes 983048 | tf_op jit(solution)/shard_map/ppermute | solution.py:65
  101.3 19.7 %collective-permute-start.25 = (bf16[1280,128]{1,0:T(8,128)(2,1)S(1)}, bf16[1280,128]{1,0:T(8,128)(2,1)S(1)}, u32[]{:S(2)}, u32[]{:S(2)}) collective-permute-start(bf16[1280,128]{1,0:T(8,128)(2,1)S(1)} %get-tuple-element.31), channel_id=1, source_target_pairs={{3,1},{7,5},{11,9},{15,13},{19,17},{23,21},{27,25},{31,29}} | collective-permute-start | bytes 983048 | tf_op jit(solution)/shard_map/ppermute | solution.py:65
  102.0 20.6 %collective-permute-start.21 = (bf16[1280,128]{1,0:T(8,128)(2,1)S(1)}, bf16[1280,128]{1,0:T(8,128)(2,1)S(1)}, u32[]{:S(2)}, u32[]{:S(2)}) collective-permute-start(bf16[1280,128]{1,0:T(8,128)(2,1)S(1)} %get-tuple-element.32), channel_id=1, source_target_pairs={{0,1},{1,2},{4,5},{5,6},{8,9},{9,10},{12,13},{13,14},{16,17},{17,1... | collective-permute-start | bytes 983048 | tf_op jit(solution)/shard_map/ppermute | solution.py:64
  112.5 22.4 %collective-permute-start.12 = (bf16[1280,128]{1,0:T(8,128)(2,1)S(1)}, bf16[1280,128]{1,0:T(8,128)(2,1)S(1)}, u32[]{:S(2)}, u32[]{:S(2)}) collective-permute-start(bf16[1280,128]{1,0:T(8,128)(2,1)S(1)} %get-tuple-element.26), channel_id=1, source_target_pairs={{2,1},{3,2},{6,5},{7,6},{10,9},{11,10},{14,13},{15,14},{18,17},{19... | collective-permute-start | bytes 983048 | tf_op jit(solution)/shard_map/ppermute | solution.py:65
  113.2 29.3 %collective-permute-start.9 = (bf16[1280,128]{1,0:T(8,128)(2,1)S(1)}, bf16[1280,128]{1,0:T(8,128)(2,1)S(1)}, u32[]{:S(2)}, u32[]{:S(2)}) collective-permute-start(bf16[1280,128]{1,0:T(8,128)(2,1)S(1)} %get-tuple-element.26), channel_id=1, source_target_pairs={{0,1},{1,2},{4,5},{5,6},{8,9},{9,10},{12,13},{13,14},{16,17},{17,1... | collective-permute-start | bytes 983048 | tf_op jit(solution)/shard_map/ppermute | solution.py:64
  117.7 15.1 %collective-permute-start.22 = (bf16[1280,128]{1,0:T(8,128)(2,1)S(1)}, bf16[1280,128]{1,0:T(8,128)(2,1)S(1)}, u32[]{:S(2)}, u32[]{:S(2)}) collective-permute-start(bf16[1280,128]{1,0:T(8,128)(2,1)S(1)} %get-tuple-element.33), channel_id=1, source_target_pairs={{0,2},{4,6},{8,10},{12,14},{16,18},{20,22},{24,26},{28,30}} | collective-permute-start | bytes 983048 | tf_op jit(solution)/shard_map/ppermute | solution.py:64
  121.1 19.3 %collective-permute-start.13 = (bf16[1280,128]{1,0:T(8,128)(2,1)S(1)}, bf16[1280,128]{1,0:T(8,128)(2,1)S(1)}, u32[]{:S(2)}, u32[]{:S(2)}) collective-permute-start(bf16[1280,128]{1,0:T(8,128)(2,1)S(1)} %get-tuple-element.25), channel_id=1, source_target_pairs={{3,1},{7,5},{11,9},{15,13},{19,17},{23,21},{27,25},{31,29}} | collective-permute-start | bytes 983048 | tf_op jit(solution)/shard_map/ppermute | solution.py:65
  122.6 19.9 %collective-permute-start.10 = (bf16[1280,128]{1,0:T(8,128)(2,1)S(1)}, bf16[1280,128]{1,0:T(8,128)(2,1)S(1)}, u32[]{:S(2)}, u32[]{:S(2)}) collective-permute-start(bf16[1280,128]{1,0:T(8,128)(2,1)S(1)} %get-tuple-element.27), channel_id=1, source_target_pairs={{0,2},{4,6},{8,10},{12,14},{16,18},{20,22},{24,26},{28,30}} | collective-permute-start | bytes 983048 | tf_op jit(solution)/shard_map/ppermute | solution.py:64
  132.7 15.2 %collective-permute-start.26 = (bf16[1280,128]{1,0:T(8,128)(2,1)}, bf16[1280,128]{1,0:T(8,128)(2,1)}, u32[]{:S(2)}, u32[]{:S(2)}) collective-permute-start(bf16[1280,128]{1,0:T(8,128)(2,1)} %add_convert_fusion), channel_id=1, source_target_pairs={{1,0},{2,1},{3,2},{5,4},{6,5},{7,6},{9,8},{10,9},{11,10},{13,12},{... | collective-permute-start | bytes 983048 | tf_op jit(solution)/shard_map/ppermute | solution.py:73
  134.9 13.1 %collective-permute-start.23 = (bf16[1280,128]{1,0:T(8,128)(2,1)}, bf16[1280,128]{1,0:T(8,128)(2,1)}, u32[]{:S(2)}, u32[]{:S(2)}) collective-permute-start(bf16[1280,128]{1,0:T(8,128)(2,1)} %add_convert_fusion.1), channel_id=1, source_target_pairs={{0,1},{1,2},{2,3},{4,5},{5,6},{6,7},{8,9},{9,10},{10,11},{12,13},{... | collective-permute-start | bytes 983048 | tf_op jit(solution)/shard_map/ppermute | solution.py:72
  141.2 12.3 %collective-permute-start.14 = (bf16[1280,128]{1,0:T(8,128)(2,1)}, bf16[1280,128]{1,0:T(8,128)(2,1)S(1)}, u32[]{:S(2)}, u32[]{:S(2)}) collective-permute-start(bf16[1280,128]{1,0:T(8,128)(2,1)} %add_convert_fusion.2), channel_id=1, source_target_pairs={{1,0},{2,1},{3,2},{5,4},{6,5},{7,6},{9,8},{10,9},{11,10},{13,12},{... | collective-permute-start | bytes 983048 | tf_op jit(solution)/shard_map/ppermute | solution.py:73
  143.4 10.1 %collective-permute-start.11 = (bf16[1280,128]{1,0:T(8,128)(2,1)}, bf16[1280,128]{1,0:T(8,128)(2,1)S(1)}, u32[]{:S(2)}, u32[]{:S(2)}) collective-permute-start(bf16[1280,128]{1,0:T(8,128)(2,1)} %add_convert_fusion.3), channel_id=1, source_target_pairs={{0,1},{1,2},{2,3},{4,5},{5,6},{6,7},{8,9},{9,10},{10,11},{12,13},{... | collective-permute-start | bytes 983048 | tf_op jit(solution)/shard_map/ppermute | solution.py:72
  159.4 7.2 %collective-permute-start.27 = (f32[128,128]{1,0:T(8,128)S(1)}, f32[128,128]{1,0:T(8,128)S(1)}, u32[]{:S(2)}, u32[]{:S(2)}) collective-permute-start(f32[128,128]{1,0:T(8,128)S(1)} %get-tuple-element.37.refs_0_), channel_id=1, source_target_pairs={{0,1},{1,2},{2,3},{3,0},{4,5},{5,6},{6,7},{7,4},{8,9},{9,10},{10,1... | collective-permute-start | bytes 196616 | tf_op jit(solution)/shard_map/ppermute | solution.py:31
  161.4 6.0 %collective-permute-start.28 = (f32[128,128]{1,0:T(8,128)S(1)}, f32[128,128]{1,0:T(8,128)S(1)}, u32[]{:S(2)}, u32[]{:S(2)}) collective-permute-start(f32[128,128]{1,0:T(8,128)S(1)} %get-tuple-element.37.refs_0_), channel_id=1, source_target_pairs={{0,2},{1,3},{2,0},{3,1},{4,6},{5,7},{6,4},{7,5},{8,10},{9,11},{10,... | collective-permute-start | bytes 196616 | tf_op jit(solution)/shard_map/ppermute | solution.py:31
  164.9 4.3 %collective-permute-start.29 = (f32[128,128]{1,0:T(8,128)S(1)}, f32[128,128]{1,0:T(8,128)S(1)}, u32[]{:S(2)}, u32[]{:S(2)}) collective-permute-start(f32[128,128]{1,0:T(8,128)S(1)} %get-tuple-element.37.refs_0_), channel_id=1, source_target_pairs={{0,3},{1,0},{2,1},{3,2},{4,7},{5,4},{6,5},{7,6},{8,11},{9,8},{10,9... | collective-permute-start | bytes 196616 | tf_op jit(solution)/shard_map/ppermute | solution.py:31
  (13 other events, 130.6 us)
